TPU v7x, 256 devices: a whole 4x4x8 slice. The times are simulated.
256 devices in a mesh: row: 8 (over y, core), col: 32 (over x, z).
Axes of the slice: x: 4, y: 4, z: 8, core: 2. Of those that a mesh axis runs over, the one named last changes fastest.
Arguments:
- columns: float32 [2048, 131072], P(None, ('row', 'col')), may hold values from -6000 to 6000
- seating: int32 [32], replicated, may hold values from 0 to 31, each once
Outputs:
- rotated: float32 [2048, 131072], P(None, ('row', 'col'))
All inputs are finite; a program needn't handle non-finite values.
Results may differ from a plain program's by a relative error of at most 0.0001.
Values sent between devices are 32-bit elements; how exact they have to be, the bound alone decides.
No kernel may reach another device: no remote copies, remote signals or barrier semaphores. Data moves between devices by JAX's collectives and lax.ppermute only.
A program may use at most 128 MiB of HBM per device.

v0:
```python
import jax
import jax.numpy as jnp
from jax import lax
from jax.sharding import PartitionSpec as P

BLOCK = 64
NS_STEPS = 5


highest = lax.Precision.HIGHEST


def rotation(pair_gram, total_rows):
    pair_width = pair_gram.shape[-1]
    frobenius = jnp.sqrt(jnp.sum(pair_gram * pair_gram, axis=(-2, -1), keepdims=True))
    current = pair_gram / frobenius
    identity = jnp.eye(pair_width, dtype=jnp.float32)
    inverse_root = jnp.broadcast_to(identity, pair_gram.shape)
    for newton_turn in range(NS_STEPS):
        factor = 1.5 * identity - 0.5 * jnp.matmul(inverse_root, current, precision=highest)
        current = jnp.matmul(current, factor, precision=highest)
        inverse_root = jnp.matmul(factor, inverse_root, precision=highest)
    return inverse_root * jnp.sqrt(total_rows / frobenius)


def pair_up(blocks, stride):
    count = blocks.shape[0]
    shaped = blocks.reshape(count // (2 * stride), 2, stride, blocks.shape[1], blocks.shape[2])
    return jnp.concatenate([shaped[:, 0], shaped[:, 1]], axis=2)


def split_pairs(rotated_pairs, stride):
    groups = rotated_pairs.shape[0]
    half_width = rotated_pairs.shape[2] // 2
    shaped = rotated_pairs.reshape(groups, stride, 2, half_width, rotated_pairs.shape[3])
    return jnp.transpose(shaped, (0, 2, 1, 3, 4)).reshape(
        groups * 2 * stride, half_width, rotated_pairs.shape[3]
    )


def body(columns, seating):
    block_count = seating.shape[0]
    rows_here = columns.shape[1]
    col_count = lax.axis_size("col")
    total_rows = float(rows_here * lax.axis_size("row") * col_count)
    seat_count = block_count // col_count
    seated = columns.reshape(block_count, BLOCK, rows_here)[seating].reshape(
        block_count * BLOCK, rows_here
    )
    current = seated.reshape(block_count, BLOCK, rows_here)
    for stride in (seat_count, block_count // 2):
        paired = pair_up(current, stride)
        partial_gram = jnp.einsum("gsam,gsbm->gsab", paired, paired, precision=highest)
        pair_gram = lax.psum(partial_gram, ("row", "col"))
        rotate = rotation(pair_gram, total_rows)
        moved = jnp.einsum("gsab,gsam->gsbm", rotate, paired, precision=highest)
        current = split_pairs(moved, stride)
    seated = current.reshape(block_count * BLOCK, rows_here)
    ordered = seated.reshape(block_count, BLOCK, rows_here)
    restored = jnp.zeros_like(ordered).at[seating].set(ordered)
    return restored.reshape(block_count * BLOCK, rows_here)


def solution(mesh):
    in_specs = (P(None, ("row", "col")), P())
    out_specs = P(None, ("row", "col"))
    return jax.shard_map(body, mesh=mesh, in_specs=in_specs, out_specs=out_specs, check_vma=False)
```

profile of v0, /device:TPU:1, one launch (start us, length us, event | category | flops | bytes accessed | tf_op | source)
XLA Modules:
  0.0 616.6 jit_solution(11122427788383581620)
XLA Ops:
  6.5 0.7 compare_select_fusion
  7.2 5.0 gather_fusion
  12.2 2.7 slice_bitcast_fusion.3
  15.0 1.3 copy-done
  16.3 5.0 fusion.4
  21.3 0.0 all-reduce.3.cloned.1.call-update
  21.3 0.5 all-reduce.5.cloned.1.call-start
  21.9 260.7 %all-reduce.3.cloned.1.call-done = f32[16,1,128,128]{3,2,0,1:T(8,128)} async-done(((f32[16,1,128,128]{3,2,0,1:T(8,128)}), f32[16,1,128,128]{3,2,0,1:T(8,128)}) %all-reduce.3.cloned.1.call-update) | async-done | bytes 1048592 | tf_op jit(solution)/shard_map/psum | solution.py:54
  282.6 1.5 multiply_reduce_fusion.1
  284.2 2.3 fusion.15
  286.5 1.0 fusion.25
  287.5 1.3 fusion.19
  288.8 1.2 fusion.14
  290.0 1.2 fusion.35
  291.2 1.2 fusion.34
  292.4 1.2 fusion.13
  293.6 1.2 fusion.37
  294.8 1.2 fusion.36
  296.0 1.4 fusion.12
  297.4 1.2 fusion.38
  298.6 1.2 fusion.39
  299.8 1.2 fusion.11
  301.0 1.9 convolution_multiply_fusion.6
  303.0 3.8 fusion.2
  306.7 0.5 slice_bitcast_fusion.1
  307.3 1.3 copy-done.2
  308.6 5.4 fusion.5
  314.0 0.0 all-reduce.5.cloned.1.call-update
  314.0 258.0 %all-reduce.5.cloned.1.call-done = f32[1,16,128,128]{3,2,1,0:T(8,128)} async-done(((f32[1,16,128,128]{3,2,1,0:T(8,128)}), f32[1,16,128,128]{3,2,1,0:T(8,128)}) %all-reduce.5.cloned.1.call-update) | async-done | bytes 1048592 | tf_op jit(solution)/shard_map/psum | solution.py:54
  572.0 1.5 multiply_reduce_fusion
  573.6 2.3 fusion.10
  575.9 1.0 fusion.22
  577.0 1.3 fusion.16
  578.2 1.2 fusion.9
  579.5 1.2 fusion.41
  580.6 1.2 fusion.40
  581.8 1.2 fusion.8
  583.1 1.2 fusion.43
  584.3 1.4 fusion.42
  585.6 1.2 fusion.7
  586.8 1.2 fusion.44
  588.0 1.2 fusion.45
  589.2 1.2 fusion.6
  590.5 1.9 convolution_multiply_fusion
  592.4 3.8 fusion
  596.1 2.6 copy.5
  598.8 2.5 broadcast_in_dim.4
  601.3 8.3 %scatter_fusion = f32[32,64,512]{2,1,0:T(8,128)} fusion(f32[32,64,512]{2,1,0:T(8,128)} %broadcast_in_dim.4, s32[32]{0:T(128)S(1)} %compare_select_fusion, f32[32,64,512]{2,1,0:T(8,128)} %bitcast.98), kind=kCustom, calls=%fused_computation.1 | custom fusion | bytes 12583040 | tf_op jit(solution)/shard_map/scatter | solution.py:60
  (16 shorter events, 0.1 us)
Async XLA Ops:
  6.5 276.1 %all-reduce.3.cloned.1.call-start = ((), (), s32[]{:S(2)}) async-start(), calls=%async_computation | async-start | bytes 2097152 | tf_op jit(solution)/shard_map/psum | solution.py:54
  15.0 1.3 copy-start
  21.3 550.7 %all-reduce.5.cloned.1.call-start = ((), (), s32[]{:S(2)}) async-start(), calls=%async_computation.1 | async-start | bytes 2097152 | tf_op jit(solution)/shard_map/psum | solution.py:54
  282.6 4.9 copy-start.4
  298.6 4.3 copy-start.1
  307.2 1.3 copy-start.2
  572.0 4.9 copy-start.5
  588.0 4.3 copy-start.3
Sparse Core Ops, SparseCore 0:
  21.4 261.1 all-reduce.2
  314.2 257.8 all-reduce.4
where the time goes:
time: 622 us; the launch traced here: 617 us
  waiting for transfers between devices  519 us (83%)
  matrix products  55.3 us (9%)
  local copies, waits for them, and re-layouts  24.4 us (4%)
  between operations  13.9 us (2%)
    psum x2, waiting for transfers between devices, body(): pair_gram = lax.psum(partial_gram, ('row', 'col'))  519 us
    dot_general x10, matrix products, rotation(): jnp.matmul(inverse_root, current, precision=highest)  14.6 us
    dot_general x10, matrix products, rotation(): inverse_root = jnp.matmul(factor, inverse_root, precision=highest)  13.1 us
  transfers between devices with their start and end apart: 2, of which 2 were waited for; matrix products, arithmetic and copies ran while one was open for 0% of the time, Pallas kernels for 0%

commit v1 on v0

v1 whole, which is shorter than its diff:
```python
import jax
import jax.numpy as jnp
from jax import lax
from jax.experimental import pallas as pl
from jax.experimental.pallas import tpu as pltpu
from jax.sharding import PartitionSpec as P

BLOCK = 64
NS_STEPS = 5
NY, NC, NX, NZ = 4, 2, 4, 8
AXES = ("row", "col")
GROUPS = 8
CHUNK = 264
HI = lax.Precision.HIGHEST


def device_permutation(move):
    pairs = []
    for y in range(NY):
        for c in range(NC):
            for x in range(NX):
                for z in range(NZ):
                    ty, tc, tx, tz = move(y, c, x, z)
                    src = (y * NC + c) * NX * NZ + x * NZ + z
                    dst = ((ty % NY) * NC + tc % NC) * NX * NZ + (tx % NX) * NZ + tz % NZ
                    pairs.append((src, dst))
    return pairs


def send(value, move):
    return lax.ppermute(value, AXES, device_permutation(move))


def swap_core(y, c, x, z):
    return y, 1 - c, x, z


def shift_y(d):
    return lambda y, c, x, z: (y + d, c, x, z)


EXCHANGES = (
    lambda y, c, x, z: (y, c, x ^ 1, z),
    lambda y, c, x, z: (y, c, NX - 1 - x, z),
    lambda y, c, x, z: (y, c, x, z ^ 1),
    lambda y, c, x, z: (y, c, x, z ^ 3),
    lambda y, c, x, z: (y, c, x, NZ - 1 - z),
)


def group_at(slot):
    me = lax.axis_index("row")
    y, c = me // NC, me % NC
    core = c if slot >= NY else 1 - c
    return lax.rem(y + slot % NY, NY) * NC + core


def seats_of(group):
    return (2 * group, 2 * group + 1, 2 * group + 16, 2 * group + 17)


def indices(shape):
    return (
        lax.broadcasted_iota(jnp.int32, shape, 0),
        lax.broadcasted_iota(jnp.int32, shape, 1),
    )


def fold(upper, lower):
    i, j = indices(upper.shape)
    diagonal = jnp.sum(jnp.where(i == j, lower, 0.0), axis=0, keepdims=True)
    return jnp.where(i <= j, upper, lower), diagonal


def unfold(folded, diagonal):
    i, j = indices(folded.shape)
    flipped = folded.T
    first = jnp.where(i <= j, folded, flipped)
    second = jnp.where(i > j, folded, jnp.where(i == j, diagonal, flipped))
    return first, second


def split2(value):
    high = value.astype(jnp.bfloat16)
    low = (value - high.astype(jnp.float32)).astype(jnp.bfloat16)
    return high, low


def dot_t(a, b):
    return lax.dot_general(a, b, (((1,), (1,)), ((), ())), preferred_element_type=jnp.float32)


def gram_kernel(seating, columns, away, home, panel, sems):
    def copies(slot):
        group = group_at(slot)
        return [
            pltpu.make_async_copy(
                columns.at[pl.ds(pl.multiple_of(seating[seat] * BLOCK, BLOCK), BLOCK), :],
                panel.at[slot, pl.ds(k * BLOCK, BLOCK), :],
                sems.at[slot, k],
            )
            for k, seat in enumerate(seats_of(group))
        ]

    started = [copies(slot) for slot in range(GROUPS)]
    for slot in range(GROUPS):
        for copy in started[slot]:
            copy.start()
    for slot in range(GROUPS):
        for copy in started[slot]:
            copy.wait()
        high, low = split2(panel[slot])
        cross = dot_t(high, low)
        gram = dot_t(high, high) + cross + dot_t(low, high)
        folded, diagonal = fold(gram[:128, :128], gram[128:, 128:])
        out = away if slot < NY else home
        out[slot % NY, 0:128, :] = gram[:128, 128:]
        out[slot % NY, 128:256, :] = folded
        out[slot % NY, 256:264, :] = jnp.broadcast_to(diagonal, (8, 128))


def mm(a, b):
    return jnp.dot(a, b, precision=HI, preferred_element_type=jnp.float32)


def rotations(grams, total_rows):
    i, j = indices((128, 128))
    identity = jnp.where(i == j, 1.0, 0.0).astype(jnp.float32)
    norms = [jnp.sqrt(jnp.sum(g * g)) for g in grams]
    currents = [g / n for g, n in zip(grams, norms)]
    factors = [1.5 * identity - 0.5 * y for y in currents]
    currents = [mm(y, f) for y, f in zip(currents, factors)]
    roots = factors
    for turn in range(1, NS_STEPS):
        products = [mm(r, y) for r, y in zip(roots, currents)]
        factors = [1.5 * identity - 0.5 * p for p in products]
        if turn + 1 < NS_STEPS:
            currents = [mm(y, f) for y, f in zip(currents, factors)]
        roots = [mm(f, r) for f, r in zip(factors, roots)]
    return [r * jnp.sqrt(total_rows / n) for r, n in zip(roots, norms)]


def stack_rows(va, vb, half):
    zero = jnp.zeros((BLOCK, 128), jnp.float32)
    rows = slice(half * BLOCK, half * BLOCK + BLOCK)
    return jnp.concatenate(
        [
            jnp.concatenate([va[rows], zero], axis=1),
            jnp.concatenate([zero, vb[rows]], axis=1),
        ],
        axis=0,
    )


def rotation_kernel(total_rows, mine, theirs, out):
    whole = mine[...] + theirs[...]
    cross = whole[0:128]
    first, second = unfold(whole[128:256], whole[256:257])
    gram = jnp.concatenate(
        [
            jnp.concatenate([first, cross], axis=1),
            jnp.concatenate([cross.T, second], axis=1),
        ],
        axis=0,
    )
    va, vb = rotations([first, second], total_rows)
    lower = stack_rows(va, vb, 0)
    upper = stack_rows(va, vb, 1)

    def turned(q):
        return lax.dot_general(
            mm(q, gram), q, (((1,), (1,)), ((), ())), precision=HI, preferred_element_type=jnp.float32
        )

    vc, vd = rotations([turned(lower), turned(upper)], total_rows)
    ab, b_diagonal = fold(va, vb)
    cd, d_diagonal = fold(vc, vd)
    out[0:128] = ab
    out[128:256] = cd
    i, _ = indices((8, 128))
    out[256:264] = jnp.where(i == 0, b_diagonal, d_diagonal)


def apply_kernel(seating, columns, *refs):
    turns = refs[:GROUPS]
    out, panel, result, in_sems, out_sems = refs[GROUPS:]

    def copies(slot):
        group = group_at(slot)
        ins, outs = [], []
        for k, seat in enumerate(seats_of(group)):
            rows = pl.ds(pl.multiple_of(seating[seat] * BLOCK, BLOCK), BLOCK)
            ins.append(
                pltpu.make_async_copy(
                    columns.at[rows, :], panel.at[slot, pl.ds(k * BLOCK, BLOCK), :], in_sems.at[slot, k]
                )
            )
        for k, seat in enumerate((2 * group, 2 * group + 16, 2 * group + 1, 2 * group + 17)):
            rows = pl.ds(pl.multiple_of(seating[seat] * BLOCK, BLOCK), BLOCK)
            outs.append(
                pltpu.make_async_copy(
                    result.at[slot, pl.ds(k * BLOCK, BLOCK), :], out.at[rows, :], out_sems.at[slot, k]
                )
            )
        return ins, outs

    order = list(range(NY, GROUPS)) + list(range(NY))
    started = {slot: copies(slot) for slot in order}
    for slot in order:
        for copy in started[slot][0]:
            copy.start()
    for slot in order:
        turn = turns[slot][...]
        va, vb = unfold(turn[0:128], turn[256:257])
        vc, vd = unfold(turn[128:256], turn[257:258])
        rotate = jnp.concatenate([mm(vc, stack_rows(va, vb, 0)), mm(vd, stack_rows(va, vb, 1))], axis=0)
        for copy in started[slot][0]:
            copy.wait()
        result[slot] = mm(rotate, panel[slot])
        for copy in started[slot][1]:
            copy.start()
    for slot in order:
        for copy in started[slot][1]:
            copy.wait()


def body(columns, seating):
    rows_here = columns.shape[1]
    total_rows = float(rows_here * lax.axis_size(AXES))
    smem = pl.BlockSpec(memory_space=pltpu.SMEM)
    hbm = pl.BlockSpec(memory_space=pl.ANY)
    vmem = pl.BlockSpec(memory_space=pltpu.VMEM)
    chunk = jax.ShapeDtypeStruct((CHUNK, 128), jnp.float32)
    quarter = jax.ShapeDtypeStruct((NY, CHUNK, 128), jnp.float32)

    away, home = pl.pallas_call(
        gram_kernel,
        out_shape=(quarter, quarter),
        in_specs=[smem, hbm],
        out_specs=(vmem, vmem),
        scratch_shapes=[
            pltpu.VMEM((GROUPS, 256, rows_here), jnp.float32),
            pltpu.SemaphoreType.DMA((GROUPS, 4)),
        ],
        name="gram",
    )(seating, columns)

    here = home + send(away, swap_core)
    arrived = [send(here[d], shift_y(d)) for d in range(1, NY)]
    total = here[0] + arrived[0] + arrived[1] + arrived[2]
    for exchange in EXCHANGES[:-1]:
        total = total + send(total, exchange)
    other = send(total, EXCHANGES[-1])

    turn = pl.pallas_call(
        lambda *refs: rotation_kernel(total_rows, *refs),
        out_shape=chunk,
        in_specs=[vmem, vmem],
        out_specs=vmem,
        name="rotation",
    )(total, other)

    near = [turn] + [send(turn, shift_y(-d)) for d in range(1, NY)]
    far = [send(t, swap_core) for t in near]

    return pl.pallas_call(
        apply_kernel,
        out_shape=jax.ShapeDtypeStruct(columns.shape, columns.dtype),
        in_specs=[smem, hbm] + [vmem] * GROUPS,
        out_specs=hbm,
        scratch_shapes=[
            pltpu.VMEM((GROUPS, 256, rows_here), jnp.float32),
            pltpu.VMEM((GROUPS, 256, rows_here), jnp.float32),
            pltpu.SemaphoreType.DMA((GROUPS, 4)),
            pltpu.SemaphoreType.DMA((GROUPS, 4)),
        ],
        name="apply",
    )(seating, columns, *far, *near)


def solution(mesh):
    in_specs = (P(None, AXES), P())
    out_specs = P(None, AXES)
    return jax.shard_map(body, mesh=mesh, in_specs=in_specs, out_specs=out_specs, check_vma=False)
```

time: 622 us -> 87 us (0.14)
  waiting for transfers between devices: 519 us -> 22.5 us
  matrix products: 55.3 us -> 0 us
  starting transfers between devices: 0.51 us -> 36 us
  Pallas kernels: 0 us -> 25.5 us
  local copies, waits for them, and re-layouts: 24.4 us -> 1.34 us
  between operations: 13.9 us -> 0.28 us
    psum x2 -> x0, waiting for transfers between devices: 519 us -> none  [body(): pair_gram = lax.psum(partial_gram, ('row', 'col'))]
    dot_general x32 -> x0, matrix products: 55.3 us -> none  [the longest x10 14.6 us: rotation(): jnp.matmul(inverse_root, current, precision=highest)]
    ppermute x0 -> x16, starting transfers between devices: none -> 36 us  [send(): return lax.ppermute(value, AXES, device_permutation(move))]
    pallas_call x0 -> x3, Pallas kernels: none -> 25.5 us  [the longest x1 10.2 us: body(): pl.pallas_call(apply_kernel, out_shape=jax.ShapeDtypeStruct(columns.shape...]
    ppermute x0 -> x16, waiting for transfers between devices: none -> 22.5 us  [send(): return lax.ppermute(value, AXES, device_permutation(move))]
    scatter x1 -> x0, local copies, waits for them, and re-layouts: 8.27 us -> none  [body(): restored = jnp.zeros_like(ordered).at[seating].set(ordered)]
  transfers between devices with their start and end apart: 2 -> 16, of which waited for: 2 -> 11; matrix products, arithmetic and copies ran while one was open for 0% -> 0% of each run, Pallas kernels for 0% -> 0%
where the time goes in v1:
time: 87 us; the launch traced here: 86.8 us
  starting transfers between devices  36 us (41%)
  Pallas kernels  25.5 us (29%)
  waiting for transfers between devices  22.5 us (26%)
  local copies, waits for them, and re-layouts  1.34 us (2%)
  other arithmetic  1.22 us (1%)
    ppermute x16, starting transfers between devices, send(): return lax.ppermute(value, AXES, device_permutation(move))  36 us
    ppermute x16, waiting for transfers between devices, send(): return lax.ppermute(value, AXES, device_permutation(move))  22.5 us
    pallas_call x1, Pallas kernels, body(): pl.pallas_call(apply_kernel, out_shape=jax.ShapeDtypeStruct(columns.shape...  10.2 us
    pallas_call x1, Pallas kernels, body(): pl.pallas_call(gram_kernel, out_shape=(quarter, quarter), in_specs=[smem,...  7.72 us
    pallas_call x1, Pallas kernels, body(): pl.pallas_call(lambda *refs: rotation_kernel(total_rows, *refs), out_shap...  7.53 us
  transfers between devices with their start and end apart: 16, of which 11 were waited for; matrix products, arithmetic and copies ran while one was open for 0% of the time, Pallas kernels for 0%

profile of v1, /device:TPU:1, one launch (start us, length us, event | category | flops | bytes accessed | tf_op | source)
XLA Modules:
  0.0 86.8 jit_solution(8955440745247068051)
XLA Ops:
  0.0 7.7 %gram.1 = (f32[4,264,128]{2,1,0:T(8,128)}, f32[4,264,128]{2,1,0:T(8,128)}) custom-call(s32[32]{0:T(128)} %seating.3, f32[2048,512]{1,0:T(8,128)} %columns.3), custom_call_target="tpu_custom_call" | custom-call | tf_op jit(solution)/shard_map/gram/pallas_call | solution.py:236
  7.7 3.3 %collective-permute-start = (f32[4,264,128]{2,1,0:T(8,128)}, f32[4,264,128]{2,1,0:T(8,128)S(1)}, u32[]{:S(2)}, u32[]{:S(2)}) collective-permute-start(f32[4,264,128]{2,1,0:T(8,128)} %get-tuple-element.8), channel_id=1, source_target_pairs={{0,32},{1,33},{2,34},{3,35},{4,36},{5,37},{6,38},{7,39},{8,40},{9,... | collective-permute-start | bytes 1622024 | tf_op jit(solution)/shard_map/ppermute | solution.py:31
  11.0 1.8 %collective-permute-done = f32[4,264,128]{2,1,0:T(8,128)S(1)} collective-permute-done((f32[4,264,128]{2,1,0:T(8,128)}, f32[4,264,128]{2,1,0:T(8,128)S(1)}, u32[]{:S(2)}, u32[]{:S(2)}) %collective-permute-start) | collective-permute-done | bytes 540704 | tf_op jit(solution)/shard_map/ppermute | solution.py:31
  12.8 1.1 %add.24 = f32[4,264,128]{2,1,0:T(8,128)S(1)} add(f32[4,264,128]{2,1,0:T(8,128)} %get-tuple-element.7, f32[4,264,128]{2,1,0:T(8,128)S(1)} %collective-permute-done) | non-fusion elementwise | flops 135168 | bytes 1622016 | tf_op jit(solution)/shard_map/add | solution.py:248
  13.9 0.1 collective-permute-start.1
  14.0 2.7 %collective-permute-start.3 = (f32[264,128]{1,0:T(8,128)S(1)}, f32[264,128]{1,0:T(8,128)S(1)}, u32[]{:S(2)}, u32[]{:S(2)}) collective-permute-start(f32[264,128]{1,0:T(8,128)S(1)} %get-tuple-element.10), channel_id=1, source_target_pairs={{0,192},{1,193},{2,194},{3,195},{4,196},{5,197},{6,198},{7,199},{8... | collective-permute-start | bytes 405512 | tf_op jit(solution)/shard_map/ppermute | solution.py:31
  16.7 0.0 collective-permute-start.2
  16.7 3.3 %collective-permute-done.1 = f32[264,128]{1,0:T(8,128)S(1)} collective-permute-done((f32[264,128]{1,0:T(8,128)S(1)}, f32[264,128]{1,0:T(8,128)S(1)}, u32[]{:S(2)}, u32[]{:S(2)}) %collective-permute-start.1) | collective-permute-done | bytes 135200 | tf_op jit(solution)/shard_map/ppermute | solution.py:31
  20.0 2.0 %collective-permute-done.3 = f32[264,128]{1,0:T(8,128)S(1)} collective-permute-done((f32[264,128]{1,0:T(8,128)S(1)}, f32[264,128]{1,0:T(8,128)S(1)}, u32[]{:S(2)}, u32[]{:S(2)}) %collective-permute-start.3) | collective-permute-done | bytes 135200 | tf_op jit(solution)/shard_map/ppermute | solution.py:31
  22.0 0.4 collective-permute-done.2
  22.4 1.3 %collective-permute-start.4 = (f32[264,128]{1,0:T(8,128)S(1)}, f32[264,128]{1,0:T(8,128)S(1)}, u32[]{:S(2)}, u32[]{:S(2)}) collective-permute-start(f32[264,128]{1,0:T(8,128)S(1)} %fusion.2), channel_id=1, source_target_pairs={{0,8},{1,9},{2,10},{3,11},{4,12},{5,13},{6,14},{7,15},{8,0},{9,1},... | collective-permute-start | bytes 405512 | tf_op jit(solution)/shard_map/ppermute | solution.py:31
  23.8 2.6 %collective-permute-done.4 = f32[264,128]{1,0:T(8,128)S(1)} collective-permute-done((f32[264,128]{1,0:T(8,128)S(1)}, f32[264,128]{1,0:T(8,128)S(1)}, u32[]{:S(2)}, u32[]{:S(2)}) %collective-permute-start.4) | collective-permute-done | bytes 135200 | tf_op jit(solution)/shard_map/ppermute | solution.py:31
  26.4 2.6 %collective-permute-start.5 = (f32[264,128]{1,0:T(8,128)S(1)}, f32[264,128]{1,0:T(8,128)S(1)}, u32[]{:S(2)}, u32[]{:S(2)}) collective-permute-start(f32[264,128]{1,0:T(8,128)S(1)} %add.28), channel_id=1, source_target_pairs={{0,24},{1,25},{2,26},{3,27},{4,28},{5,29},{6,30},{7,31},{8,16},{9,... | collective-permute-start | bytes 405512 | tf_op jit(solution)/shard_map/ppermute | solution.py:31
  29.0 2.6 %collective-permute-done.5 = f32[264,128]{1,0:T(8,128)S(1)} collective-permute-done((f32[264,128]{1,0:T(8,128)S(1)}, f32[264,128]{1,0:T(8,128)S(1)}, u32[]{:S(2)}, u32[]{:S(2)}) %collective-permute-start.5) | collective-permute-done | bytes 135200 | tf_op jit(solution)/shard_map/ppermute | solution.py:31
  31.6 1.7 %collective-permute-start.6 = (f32[264,128]{1,0:T(8,128)S(1)}, f32[264,128]{1,0:T(8,128)S(1)}, u32[]{:S(2)}, u32[]{:S(2)}) collective-permute-start(f32[264,128]{1,0:T(8,128)S(1)} %add.29), channel_id=1, source_target_pairs={{0,1},{1,0},{2,3},{3,2},{4,5},{5,4},{6,7},{7,6},{8,9},{9,8},{10,11... | collective-permute-start | bytes 405512 | tf_op jit(solution)/shard_map/ppermute | solution.py:31
  33.3 2.4 %collective-permute-done.6 = f32[264,128]{1,0:T(8,128)S(1)} collective-permute-done((f32[264,128]{1,0:T(8,128)S(1)}, f32[264,128]{1,0:T(8,128)S(1)}, u32[]{:S(2)}, u32[]{:S(2)}) %collective-permute-start.6) | collective-permute-done | bytes 135200 | tf_op jit(solution)/shard_map/ppermute | solution.py:31
  35.8 4.3 %collective-permute-start.7 = (f32[264,128]{1,0:T(8,128)S(1)}, f32[264,128]{1,0:T(8,128)S(1)}, u32[]{:S(2)}, u32[]{:S(2)}) collective-permute-start(f32[264,128]{1,0:T(8,128)S(1)} %add.30), channel_id=1, source_target_pairs={{0,3},{1,2},{2,1},{3,0},{4,7},{5,6},{6,5},{7,4},{8,11},{9,10},{10,... | collective-permute-start | bytes 405512 | tf_op jit(solution)/shard_map/ppermute | solution.py:31
  40.0 3.7 %collective-permute-done.7 = f32[264,128]{1,0:T(8,128)S(1)} collective-permute-done((f32[264,128]{1,0:T(8,128)S(1)}, f32[264,128]{1,0:T(8,128)S(1)}, u32[]{:S(2)}, u32[]{:S(2)}) %collective-permute-start.7) | collective-permute-done | bytes 135200 | tf_op jit(solution)/shard_map/ppermute | solution.py:31
  43.7 0.0 copy-start
  43.7 4.0 %collective-permute-start.8 = (f32[264,128]{1,0:T(8,128)S(1)}, f32[264,128]{1,0:T(8,128)S(1)}, u32[]{:S(2)}, u32[]{:S(2)}) collective-permute-start(f32[264,128]{1,0:T(8,128)S(1)} %add.31.refs_0_), channel_id=1, source_target_pairs={{0,7},{1,6},{2,5},{3,4},{4,3},{5,2},{6,1},{7,0},{8,15},{9,14},{10,... | collective-permute-start | bytes 405512 | tf_op jit(solution)/shard_map/ppermute | solution.py:31
  47.8 2.8 %collective-permute-done.8.refs_1_ = f32[264,128]{1,0:T(8,128)S(1)} collective-permute-done((f32[264,128]{1,0:T(8,128)S(1)}, f32[264,128]{1,0:T(8,128)S(1)}, u32[]{:S(2)}, u32[]{:S(2)}) %collective-permute-start.8) | collective-permute-done | bytes 135200 | tf_op jit(solution)/shard_map/ppermute | solution.py:31
  50.6 0.0 copy-done
  50.6 0.6 copy-done.1
  51.2 7.5 %rotation.1.refs_4_ = f32[264,128]{1,0:T(8,128)} custom-call(f32[264,128]{1,0:T(8,128)} %copy-done, f32[264,128]{1,0:T(8,128)} %copy-done.1), custom_call_target="tpu_custom_call" | custom-call | tf_op jit(solution)/shard_map/rotation/pallas_call | solution.py:255
  58.7 0.6 collective-permute-start.14
  59.3 1.9 %collective-permute-start.12 = (f32[264,128]{1,0:T(8,128)}, f32[264,128]{1,0:T(8,128)S(1)}, u32[]{:S(2)}, u32[]{:S(2)}) collective-permute-start(f32[264,128]{1,0:T(8,128)} %rotation.1.refs_4_), channel_id=1, source_target_pairs={{0,128},{1,129},{2,130},{3,131},{4,132},{5,133},{6,134},{7,135},{8... | collective-permute-start | bytes 405512 | tf_op jit(solution)/shard_map/ppermute | solution.py:31
  61.2 0.4 collective-permute-start.10
  61.7 8.7 %collective-permute-start.9 = (f32[264,128]{1,0:T(8,128)}, f32[264,128]{1,0:T(8,128)S(1)}, u32[]{:S(2)}, u32[]{:S(2)}) collective-permute-start(f32[264,128]{1,0:T(8,128)} %rotation.1.refs_4_), channel_id=1, source_target_pairs={{0,32},{1,33},{2,34},{3,35},{4,36},{5,37},{6,38},{7,39},{8,40},{9,... | collective-permute-start | bytes 405512 | tf_op jit(solution)/shard_map/ppermute | solution.py:31
  70.4 0.0 collective-permute-done.14.refs_7_
  70.4 2.0 %collective-permute-start.15 = (f32[264,128]{1,0:T(8,128)S(1)}, f32[264,128]{1,0:T(8,128)S(1)}, u32[]{:S(2)}, u32[]{:S(2)}) collective-permute-start(f32[264,128]{1,0:T(8,128)S(1)} %collective-permute-done.14.refs_7_), channel_id=1, source_target_pairs={{0,32},{1,33},{2,34},{3,35},{4,36},{5,37},{6,38},{7,39},{8,40},{9,... | collective-permute-start | bytes 405512 | tf_op jit(solution)/shard_map/ppermute | solution.py:31
  72.5 0.0 collective-permute-done.12.refs_6_
  72.5 1.5 %collective-permute-start.13 = (f32[264,128]{1,0:T(8,128)S(1)}, f32[264,128]{1,0:T(8,128)S(1)}, u32[]{:S(2)}, u32[]{:S(2)}) collective-permute-start(f32[264,128]{1,0:T(8,128)S(1)} %collective-permute-done.12.refs_6_), channel_id=1, source_target_pairs={{0,32},{1,33},{2,34},{3,35},{4,36},{5,37},{6,38},{7,39},{8,40},{9,... | collective-permute-start | bytes 405512 | tf_op jit(solution)/shard_map/ppermute | solution.py:31
  74.0 0.0 collective-permute-done.10.refs_5_
  74.0 0.7 collective-permute-start.11
  74.8 0.0 collective-permute-done.9.refs_0_
  74.8 0.0 collective-permute-done.15.refs_3_
  74.8 0.0 copy-start.6
  74.8 0.2 collective-permute-done.13.refs_2_
  75.0 0.8 collective-permute-done.11.refs_1_
  75.8 0.0 copy-done.2
  75.8 0.0 copy-done.3
  75.8 0.0 copy-done.4
  75.8 0.0 copy-done.5
  75.8 0.0 copy-done.6
  75.8 0.0 copy-done.7
  75.8 0.0 copy-start.8
  75.8 0.6 copy-done.8
  76.4 10.2 %apply.1 = f32[2048,512]{1,0:T(8,128)} custom-call(s32[32]{0:T(128)} %seating.3, f32[2048,512]{1,0:T(8,128)} %columns.3, f32[264,128]{1,0:T(8,128)} %copy-done.5, f32[264,128]{1,0:T(8,128)} %copy-done.8, f32[264,128]{1,0:T(8,128)} %copy-done.7, f32[264,128]{1,0:T(8,128)} %copy-done.6, f32[264,128]{1,0:T(8,128)} %rotation.1.refs_4_, f32[264,128]{1,0:T(8,128)} %copy-done.4, ...), custom_call_target="tpu_custom_call" | custom-call | tf_op jit(solution)/shard_map/apply/pallas_call | solution.py:266
  (12 shorter events, 0.2 us)
Async XLA Ops:
  7.7 5.1 %collective-permute-start = (f32[4,264,128]{2,1,0:T(8,128)}, f32[4,264,128]{2,1,0:T(8,128)S(1)}, u32[]{:S(2)}, u32[]{:S(2)}) collective-permute-start(f32[4,264,128]{2,1,0:T(8,128)} %get-tuple-element.8), channel_id=1, source_target_pairs={{0,32},{1,33},{2,34},{3,35},{4,36},{5,37},{6,38},{7,39},{8,40},{9,... | collective-permute-start | bytes 1622024 | tf_op jit(solution)/shard_map/ppermute | solution.py:31
  13.9 6.1 %collective-permute-start.1 = (f32[264,128]{1,0:T(8,128)S(1)}, f32[264,128]{1,0:T(8,128)S(1)}, u32[]{:S(2)}, u32[]{:S(2)}) collective-permute-start(f32[264,128]{1,0:T(8,128)S(1)} %get-tuple-element.9), channel_id=1, source_target_pairs={{0,64},{1,65},{2,66},{3,67},{4,68},{5,69},{6,70},{7,71},{8,72},{9,... | collective-permute-start | bytes 405512 | tf_op jit(solution)/shard_map/ppermute | solution.py:31
  14.0 7.9 %collective-permute-start.3 = (f32[264,128]{1,0:T(8,128)S(1)}, f32[264,128]{1,0:T(8,128)S(1)}, u32[]{:S(2)}, u32[]{:S(2)}) collective-permute-start(f32[264,128]{1,0:T(8,128)S(1)} %get-tuple-element.10), channel_id=1, source_target_pairs={{0,192},{1,193},{2,194},{3,195},{4,196},{5,197},{6,198},{7,199},{8... | collective-permute-start | bytes 405512 | tf_op jit(solution)/shard_map/ppermute | solution.py:31
  16.7 5.7 %collective-permute-start.2 = (f32[264,128]{1,0:T(8,128)S(1)}, f32[264,128]{1,0:T(8,128)S(1)}, u32[]{:S(2)}, u32[]{:S(2)}) collective-permute-start(f32[264,128]{1,0:T(8,128)S(1)} %get-tuple-element.11), channel_id=1, source_target_pairs={{0,128},{1,129},{2,130},{3,131},{4,132},{5,133},{6,134},{7,135},{8... | collective-permute-start | bytes 405512 | tf_op jit(solution)/shard_map/ppermute | solution.py:31
  22.4 3.9 %collective-permute-start.4 = (f32[264,128]{1,0:T(8,128)S(1)}, f32[264,128]{1,0:T(8,128)S(1)}, u32[]{:S(2)}, u32[]{:S(2)}) collective-permute-start(f32[264,128]{1,0:T(8,128)S(1)} %fusion.2), channel_id=1, source_target_pairs={{0,8},{1,9},{2,10},{3,11},{4,12},{5,13},{6,14},{7,15},{8,0},{9,1},... | collective-permute-start | bytes 405512 | tf_op jit(solution)/shard_map/ppermute | solution.py:31
  26.4 5.2 %collective-permute-start.5 = (f32[264,128]{1,0:T(8,128)S(1)}, f32[264,128]{1,0:T(8,128)S(1)}, u32[]{:S(2)}, u32[]{:S(2)}) collective-permute-start(f32[264,128]{1,0:T(8,128)S(1)} %add.28), channel_id=1, source_target_pairs={{0,24},{1,25},{2,26},{3,27},{4,28},{5,29},{6,30},{7,31},{8,16},{9,... | collective-permute-start | bytes 405512 | tf_op jit(solution)/shard_map/ppermute | solution.py:31
  31.6 4.1 %collective-permute-start.6 = (f32[264,128]{1,0:T(8,128)S(1)}, f32[264,128]{1,0:T(8,128)S(1)}, u32[]{:S(2)}, u32[]{:S(2)}) collective-permute-start(f32[264,128]{1,0:T(8,128)S(1)} %add.29), channel_id=1, source_target_pairs={{0,1},{1,0},{2,3},{3,2},{4,5},{5,4},{6,7},{7,6},{8,9},{9,8},{10,11... | collective-permute-start | bytes 405512 | tf_op jit(solution)/shard_map/ppermute | solution.py:31
  35.8 7.9 %collective-permute-start.7 = (f32[264,128]{1,0:T(8,128)S(1)}, f32[264,128]{1,0:T(8,128)S(1)}, u32[]{:S(2)}, u32[]{:S(2)}) collective-permute-start(f32[264,128]{1,0:T(8,128)S(1)} %add.30), channel_id=1, source_target_pairs={{0,3},{1,2},{2,1},{3,0},{4,7},{5,6},{6,5},{7,4},{8,11},{9,10},{10,... | collective-permute-start | bytes 405512 | tf_op jit(solution)/shard_map/ppermute | solution.py:31
  43.7 6.8 %copy-start = (f32[264,128]{1,0:T(8,128)}, f32[264,128]{1,0:T(8,128)S(1)}, u32[]{:S(2)}) copy-start(f32[264,128]{1,0:T(8,128)S(1)} %add.31.refs_0_) | copy-start | bytes 405508
  43.7 6.8 %collective-permute-start.8 = (f32[264,128]{1,0:T(8,128)S(1)}, f32[264,128]{1,0:T(8,128)S(1)}, u32[]{:S(2)}, u32[]{:S(2)}) collective-permute-start(f32[264,128]{1,0:T(8,128)S(1)} %add.31.refs_0_), channel_id=1, source_target_pairs={{0,7},{1,6},{2,5},{3,4},{4,3},{5,2},{6,1},{7,0},{8,15},{9,14},{10,... | collective-permute-start | bytes 405512 | tf_op jit(solution)/shard_map/ppermute | solution.py:31
  50.6 0.6 copy-start.1
  58.7 11.7 %collective-permute-start.14 = (f32[264,128]{1,0:T(8,128)}, f32[264,128]{1,0:T(8,128)S(1)}, u32[]{:S(2)}, u32[]{:S(2)}) collective-permute-start(f32[264,128]{1,0:T(8,128)} %rotation.1.refs_4_), channel_id=1, source_target_pairs={{0,64},{1,65},{2,66},{3,67},{4,68},{5,69},{6,70},{7,71},{8,72},{9,... | collective-permute-start | bytes 405512 | tf_op jit(solution)/shard_map/ppermute | solution.py:31
  59.3 13.2 %collective-permute-start.12 = (f32[264,128]{1,0:T(8,128)}, f32[264,128]{1,0:T(8,128)S(1)}, u32[]{:S(2)}, u32[]{:S(2)}) collective-permute-start(f32[264,128]{1,0:T(8,128)} %rotation.1.refs_4_), channel_id=1, source_target_pairs={{0,128},{1,129},{2,130},{3,131},{4,132},{5,133},{6,134},{7,135},{8... | collective-permute-start | bytes 405512 | tf_op jit(solution)/shard_map/ppermute | solution.py:31
  61.2 12.8 %collective-permute-start.10 = (f32[264,128]{1,0:T(8,128)}, f32[264,128]{1,0:T(8,128)S(1)}, u32[]{:S(2)}, u32[]{:S(2)}) collective-permute-start(f32[264,128]{1,0:T(8,128)} %rotation.1.refs_4_), channel_id=1, source_target_pairs={{0,192},{1,193},{2,194},{3,195},{4,196},{5,197},{6,198},{7,199},{8... | collective-permute-start | bytes 405512 | tf_op jit(solution)/shard_map/ppermute | solution.py:31
  61.7 13.1 %collective-permute-start.9 = (f32[264,128]{1,0:T(8,128)}, f32[264,128]{1,0:T(8,128)S(1)}, u32[]{:S(2)}, u32[]{:S(2)}) collective-permute-start(f32[264,128]{1,0:T(8,128)} %rotation.1.refs_4_), channel_id=1, source_target_pairs={{0,32},{1,33},{2,34},{3,35},{4,36},{5,37},{6,38},{7,39},{8,40},{9,... | collective-permute-start | bytes 405512 | tf_op jit(solution)/shard_map/ppermute | solution.py:31
  70.4 5.3 %copy-start.2 = (f32[264,128]{1,0:T(8,128)}, f32[264,128]{1,0:T(8,128)S(1)}, u32[]{:S(2)}) copy-start(f32[264,128]{1,0:T(8,128)S(1)} %collective-permute-done.14.refs_7_) | copy-start | bytes 405508
  70.4 4.3 %collective-permute-start.15 = (f32[264,128]{1,0:T(8,128)S(1)}, f32[264,128]{1,0:T(8,128)S(1)}, u32[]{:S(2)}, u32[]{:S(2)}) collective-permute-start(f32[264,128]{1,0:T(8,128)S(1)} %collective-permute-done.14.refs_7_), channel_id=1, source_target_pairs={{0,32},{1,33},{2,34},{3,35},{4,36},{5,37},{6,38},{7,39},{8,40},{9,... | collective-permute-start | bytes 405512 | tf_op jit(solution)/shard_map/ppermute | solution.py:31
  72.5 3.3 %copy-start.3 = (f32[264,128]{1,0:T(8,128)}, f32[264,128]{1,0:T(8,128)S(1)}, u32[]{:S(2)}) copy-start(f32[264,128]{1,0:T(8,128)S(1)} %collective-permute-done.12.refs_6_) | copy-start | bytes 405508
  72.5 2.5 %collective-permute-start.13 = (f32[264,128]{1,0:T(8,128)S(1)}, f32[264,128]{1,0:T(8,128)S(1)}, u32[]{:S(2)}, u32[]{:S(2)}) collective-permute-start(f32[264,128]{1,0:T(8,128)S(1)} %collective-permute-done.12.refs_6_), channel_id=1, source_target_pairs={{0,32},{1,33},{2,34},{3,35},{4,36},{5,37},{6,38},{7,39},{8,40},{9,... | collective-permute-start | bytes 405512 | tf_op jit(solution)/shard_map/ppermute | solution.py:31
  74.0 1.7 %copy-start.4 = (f32[264,128]{1,0:T(8,128)}, f32[264,128]{1,0:T(8,128)S(1)}, u32[]{:S(2)}) copy-start(f32[264,128]{1,0:T(8,128)S(1)} %collective-permute-done.10.refs_5_) | copy-start | bytes 405508
  74.0 1.7 %collective-permute-start.11 = (f32[264,128]{1,0:T(8,128)S(1)}, f32[264,128]{1,0:T(8,128)S(1)}, u32[]{:S(2)}, u32[]{:S(2)}) collective-permute-start(f32[264,128]{1,0:T(8,128)S(1)} %collective-permute-done.10.refs_5_), channel_id=1, source_target_pairs={{0,32},{1,33},{2,34},{3,35},{4,36},{5,37},{6,38},{7,39},{8,40},{9,... | collective-permute-start | bytes 405512 | tf_op jit(solution)/shard_map/ppermute | solution.py:31
  74.8 1.0 %copy-start.5 = (f32[264,128]{1,0:T(8,128)}, f32[264,128]{1,0:T(8,128)S(1)}, u32[]{:S(2)}) copy-start(f32[264,128]{1,0:T(8,128)S(1)} %collective-permute-done.9.refs_0_) | copy-start | bytes 405508
  74.8 1.0 %copy-start.6 = (f32[264,128]{1,0:T(8,128)}, f32[264,128]{1,0:T(8,128)S(1)}, u32[]{:S(2)}) copy-start(f32[264,128]{1,0:T(8,128)S(1)} %collective-permute-done.15.refs_3_) | copy-start | bytes 405508
  75.0 0.8 copy-start.7
  75.8 0.7 copy-start.8

commit v2 on v0

v2 whole, which is shorter than its diff:
```python
import functools

import jax
import jax.numpy as jnp
from jax import lax
from jax.experimental import pallas as pl
from jax.experimental.pallas import tpu as pltpu
from jax.sharding import PartitionSpec as P


BLOCK = 64
NS_STEPS = 5
NY, NC, NX, NZ = 4, 2, 4, 8
AXES = ("row", "col")
SPREAD = 4
CHUNK = 264
CUT = 136
MIB = 1 << 20
GRAM_MIB = 8
SPLIT_MIB = 8


def device_permutation(move):
    pairs = []
    for y in range(NY):
        for c in range(NC):
            for x in range(NX):
                for z in range(NZ):
                    ty, tc, tx, tz = move(y, c, x, z)
                    src = (y * NC + c) * NX * NZ + x * NZ + z
                    dst = ((ty % NY) * NC + tc % NC) * NX * NZ + (tx % NX) * NZ + tz % NZ
                    pairs.append((src, dst))
    return pairs


def send(value, move):
    return lax.ppermute(value, AXES, device_permutation(move))


def swap_core(y, c, x, z):
    return y, 1 - c, x, z


def shift(d):
    return lambda y, c, x, z: (y + d, c, x, z) if c == 0 else (y, c, x + d, z)


def pairings(axis):
    return {
        "x": (lambda y, c, x, z: (y, c, x ^ 1, z), lambda y, c, x, z: (y, c, NX - 1 - x, z)),
        "y": (lambda y, c, x, z: (y ^ 1, c, x, z), lambda y, c, x, z: (NY - 1 - y, c, x, z)),
        "z": (
            lambda y, c, x, z: (y, c, x, z ^ 1),
            lambda y, c, x, z: (y, c, x, z ^ 3),
            lambda y, c, x, z: (y, c, x, NZ - 1 - z),
        ),
    }[axis]


def by_core(first, second):
    return lambda y, c, x, z: first(y, c, x, z) if c == 0 else second(y, c, x, z)


EXCHANGES = tuple(
    by_core(first, second)
    for first, second in (
        *zip(pairings("x") + pairings("z"), pairings("z") + pairings("y")),
        *zip(pairings("z") + pairings("x"), pairings("y") + pairings("z")),
    )
)


def group_at(slot):
    row = lax.axis_index("row")
    y, c = row // NC, row % NC
    x = lax.axis_index("col") // NZ
    mine = slot >= SPREAD
    place = y * (1 - c) + x * c if mine else x * (1 - c) + y * c
    return lax.rem(place + slot % SPREAD, SPREAD) * NC + (c if mine else 1 - c)


def seat_rows(seating, seat):
    return pl.ds(pl.multiple_of(seating[seat] * BLOCK, BLOCK), BLOCK)


def blocks_of(slot):
    group = group_at(slot)
    return 2 * group, 2 * group + 1, 2 * group + 16, 2 * group + 17


def indices(shape):
    return (
        lax.broadcasted_iota(jnp.int32, shape, 0),
        lax.broadcasted_iota(jnp.int32, shape, 1),
    )


def fold(upper, lower):
    i, j = indices(upper.shape)
    diagonal = jnp.sum(jnp.where(i == j, lower, 0.0), axis=0, keepdims=True)
    return jnp.where(i <= j, upper, lower), diagonal


def unfold(folded, diagonal):
    i, j = indices(folded.shape)
    flipped = folded.T
    first = jnp.where(i <= j, folded, flipped)
    second = jnp.where(i > j, folded, jnp.where(i == j, diagonal, flipped))
    return first, second


def pieces(value):
    high = value.astype(jnp.bfloat16)
    rest = value - high.astype(jnp.float32)
    middle = rest.astype(jnp.bfloat16)
    low = (rest - middle.astype(jnp.float32)).astype(jnp.bfloat16)
    return high, middle, low


def wide(parts, axis):
    high, middle, low = parts
    if axis == 1:
        return jnp.concatenate([high, high, middle, middle, high, low], axis=1)
    return jnp.concatenate([high, middle, high, middle, low, high], axis=0)


def mm(a, b):
    return jnp.dot(wide(a, 1), wide(b, 0), preferred_element_type=jnp.float32)


def dot_t(a, b):
    return lax.dot_general(a, b, (((1,), (1,)), ((), ())), preferred_element_type=jnp.float32)


def mm_t(a, b):
    left = wide(a, 1)
    high, middle, low = b
    return dot_t(left, jnp.concatenate([high, middle, high, middle, low, high], axis=1))


def gram_kernel(first_slot, whole, seating, columns, *outs):
    for k in range(SPREAD):
        seats = blocks_of(first_slot + k)
        value = jnp.concatenate([columns[seat_rows(seating, seat), :] for seat in seats], axis=0)
        high = value.astype(jnp.bfloat16)
        low = (value - high.astype(jnp.float32)).astype(jnp.bfloat16)
        both = dot_t(jnp.concatenate([high, low], axis=0), high)
        even, odd = both[:256], both[256:]
        upper = even[:128, :128] + odd[:128, :128] + odd[:128, :128].T
        cross = even[:128, 128:] + odd[:128, 128:] + odd[128:, :128].T
        lower = even[128:, 128:] + odd[128:, 128:] + odd[128:, 128:].T
        folded, diagonal = fold(upper, lower)
        out = outs[0].at[k] if whole else outs[k]
        out[0:128, :] = folded
        out[128:136, :] = jnp.broadcast_to(diagonal, (8, 128))
        out[136:264, :] = cross


def rotations(grams, total_rows):
    i, j = indices((128, 128))
    identity = jnp.where(i == j, 1.0, 0.0).astype(jnp.float32)
    squares = [jnp.sum(jnp.sum(g * g, axis=0, keepdims=True), axis=1, keepdims=True) for g in grams]
    inverses = [1.0 / jnp.sqrt(s) for s in squares]
    currents = [g * v for g, v in zip(grams, inverses)]
    factors = [1.5 * identity - 0.5 * y for y in currents]
    factors = [pieces(f) for f in factors]
    currents = [mm(pieces(y), f) for y, f in zip(currents, factors)]
    root_pieces = factors
    for turn in range(1, NS_STEPS):
        current_pieces = [pieces(y) for y in currents]
        products = [mm(r, y) for r, y in zip(root_pieces, current_pieces)]
        factors = [pieces(1.5 * identity - 0.5 * p) for p in products]
        if turn + 1 < NS_STEPS:
            joint = [
                mm(f, tuple(jnp.concatenate([p, q], axis=1) for p, q in zip(y, r)))
                for f, y, r in zip(factors, current_pieces, root_pieces)
            ]
            currents = [j[:, :128] for j in joint]
            root_pieces = [pieces(j[:, 128:]) for j in joint]
        else:
            roots = [mm(f, r) for f, r in zip(factors, root_pieces)]
    return [r * jnp.sqrt(total_rows * v) for r, v in zip(roots, inverses)]


def stack_rows(va, vb, half):
    zero = jnp.zeros((BLOCK, 128), va.dtype)
    rows = slice(half * BLOCK, half * BLOCK + BLOCK)
    return jnp.concatenate(
        [
            jnp.concatenate([va[rows], zero], axis=1),
            jnp.concatenate([zero, vb[rows]], axis=1),
        ],
        axis=0,
    )


def rotation_kernel(total_rows, straight, crossed, out):
    first, second = unfold(straight[0:128], straight[128:129])
    cross = crossed[...]
    va, vb = rotations([first, second], total_rows)
    pa, pb = pieces(va), pieces(vb)
    top = mm(pa, pieces(jnp.concatenate([first, cross], axis=1)))
    bottom = mm(pb, pieces(jnp.concatenate([cross.T, second], axis=1)))
    grams = []
    for half in range(2):
        rows = slice(half * BLOCK, half * BLOCK + BLOCK)
        left = pieces(jnp.concatenate([top[rows], bottom[rows]], axis=0))
        right = tuple(stack_rows(p, q, half) for p, q in zip(pa, pb))
        grams.append(mm_t(left, right))
    vc, vd = rotations(grams, total_rows)
    ab, b_diagonal = fold(va, vb)
    cd, d_diagonal = fold(vc, vd)
    out[0:128] = ab
    out[128:256] = cd
    i, _ = indices((8, 128))
    out[256:264] = jnp.where(i == 0, b_diagonal, d_diagonal)


def split_kernel(seating, columns, *outs):
    for slot in range(2 * SPREAD):
        for n, seat in enumerate(blocks_of(slot)):
            for part, value in enumerate(pieces(columns[seat_rows(seating, seat), :])):
                outs[slot][pl.ds(part * 256 + n * BLOCK, BLOCK), :] = value


def turned(turn, panel):
    va, vb = unfold(turn[0:128], turn[256:257])
    vc, vd = unfold(turn[128:256], turn[257:258])
    pa, pb = pieces(va), pieces(vb)
    rotate = jnp.concatenate(
        [
            mm(pieces(v), tuple(stack_rows(p, q, half) for p, q in zip(pa, pb)))
            for half, v in enumerate((vc, vd))
        ],
        axis=0,
    )
    return mm(pieces(rotate), (panel[0:256], panel[256:512], panel[512:768]))


def near_kernel(*refs):
    count = len(refs) // 3
    turns, panels, outs = refs[:count], refs[count : 2 * count], refs[2 * count :]
    for turn, panel, out in zip(turns, panels, outs):
        out[...] = turned(turn[...], panel[...])


def far_kernel(seating, *refs):
    turns, panels, done = refs[:SPREAD], refs[SPREAD : 2 * SPREAD], refs[2 * SPREAD : 3 * SPREAD]
    out, result, sems = refs[3 * SPREAD :]

    def stores(slot, value):
        group = group_at(slot)
        return [
            pltpu.make_async_copy(
                value.at[pl.ds(n * BLOCK, BLOCK), :], out.at[seat_rows(seating, seat), :], sems.at[slot, n]
            )
            for n, seat in enumerate((2 * group, 2 * group + 16, 2 * group + 1, 2 * group + 17))
        ]

    copies = []
    for k in range(SPREAD):
        copies += stores(SPREAD + k, done[k])
    for copy in copies:
        copy.start()
    for k in range(SPREAD):
        result[k] = turned(turns[k][...], panels[k][...])
        for copy in stores(k, result.at[k]):
            copy.start()
            copies.append(copy)
    for copy in copies:
        copy.wait()


def exchange(value, order):
    for axis in order:
        value = value + send(value, EXCHANGES[axis])
    return value


def steps(columns, seating):
    rows_here = columns.shape[1]
    total_rows = float(rows_here * lax.axis_size(AXES))
    smem = pl.BlockSpec(memory_space=pltpu.SMEM)
    hbm = pl.BlockSpec(memory_space=pltpu.MemorySpace.HBM)
    vmem = pl.BlockSpec(memory_space=pltpu.VMEM)
    chunk = jax.ShapeDtypeStruct((CHUNK, 128), jnp.float32)
    quarter = jax.ShapeDtypeStruct((SPREAD, CHUNK, 128), jnp.float32)
    panel_flops = 2 * 256 * 256 * rows_here

    def params(mib):
        return pltpu.CompilerParams(vmem_limit_bytes=mib * MIB)

    def cost(flops, moved):
        return pl.CostEstimate(flops=flops, bytes_accessed=moved, transcendentals=0)

    def gram(first_slot, whole):
        return pl.pallas_call(
            functools.partial(gram_kernel, first_slot, whole),
            out_shape=quarter if whole else (chunk,) * SPREAD,
            in_specs=[smem, vmem],
            out_specs=vmem if whole else (vmem,) * SPREAD,
            compiler_params=params(GRAM_MIB),
            cost_estimate=cost(2 * SPREAD * panel_flops, 2 * MIB),
            name="gram_away" if whole else "gram_home",
        )(seating, columns)

    away = gram(0, True)
    passed = send(away, swap_core)
    home = gram(SPREAD, False)
    here = [home[d] + passed[d] for d in range(SPREAD)]

    later, here = lax.optimization_barrier((seating, here))
    panels = pl.pallas_call(
        split_kernel,
        out_shape=(jax.ShapeDtypeStruct((768, rows_here), jnp.bfloat16),) * (2 * SPREAD),
        in_specs=[smem, vmem],
        out_specs=(vmem,) * (2 * SPREAD),
        compiler_params=params(SPLIT_MIB),
        cost_estimate=cost(0, 10 * MIB),
        name="split",
    )(later, columns)
    arrived = []
    for d in range(1, SPREAD):
        arrived.append(send(here[d], shift(d)))
    total = here[0] + arrived[0] + arrived[1] + arrived[2]
    total, panels = lax.optimization_barrier((total, panels))

    halves = [exchange(total[:CUT], (0, 1, 2, 3, 4)), exchange(total[CUT:], (5, 6, 7, 8, 9))]
    turn = pl.pallas_call(
        functools.partial(rotation_kernel, total_rows),
        out_shape=chunk,
        in_specs=[vmem, vmem],
        out_specs=vmem,
        compiler_params=params(8),
        name="rotation",
    )(*halves)

    def apply(slots, turns):
        count = len(slots)
        return pl.pallas_call(
            near_kernel,
            out_shape=(jax.ShapeDtypeStruct((256, rows_here), jnp.float32),) * count,
            in_specs=[vmem] * (2 * count),
            out_specs=(vmem,) * count,
            compiler_params=params(8),
            cost_estimate=cost(6 * count * panel_flops, count * MIB),
            name="apply_near",
        )(*turns, *[panels[slot] for slot in slots])

    near = [turn]
    for d in range(1, SPREAD):
        near.append(send(turn, shift(-d)))
    far = []
    for d in range(SPREAD):
        far.append(send(near[d], swap_core))
    done = apply((4,), near[:1])
    done += apply((5,), near[1:2])
    done += apply((6, 7), near[2:])
    return pl.pallas_call(
        far_kernel,
        out_shape=jax.ShapeDtypeStruct(columns.shape, columns.dtype),
        in_specs=[smem] + [vmem] * (3 * SPREAD),
        out_specs=hbm,
        scratch_shapes=[
            pltpu.VMEM((SPREAD, 256, rows_here), jnp.float32),
            pltpu.SemaphoreType.DMA((2 * SPREAD, 4)),
        ],
        compiler_params=params(10),
        name="apply_far",
    )(seating, *far, *[panels[slot] for slot in range(SPREAD)], *done)


def solution(mesh):
    in_specs = (P(None, AXES), P())
    out_specs = P(None, AXES)
    return jax.shard_map(steps, mesh=mesh, in_specs=in_specs, out_specs=out_specs, check_vma=False)
```

time: 622 us -> 71.7 us (0.12)
  waiting for transfers between devices: 519 us -> 11.9 us
  matrix products: 55.3 us -> 0 us
  starting transfers between devices: 0.51 us -> 39.7 us
  local copies, waits for them, and re-layouts: 24.4 us -> 2.86 us
  Pallas kernels: 0 us -> 16.6 us
  between operations: 13.9 us -> 0.32 us
    psum x2 -> x0, waiting for transfers between devices: 519 us -> none  [body(): pair_gram = lax.psum(partial_gram, ('row', 'col'))]
    dot_general x32 -> x0, matrix products: 55.3 us -> none  [the longest x10 14.6 us: rotation(): jnp.matmul(inverse_root, current, precision=highest)]
    ppermute x0 -> x21, starting transfers between devices: none -> 39.7 us  [send(): return lax.ppermute(value, AXES, device_permutation(move))]
    pallas_call x0 -> x8, Pallas kernels: none -> 16.6 us  [the longest x1 4.55 us: steps(): pl.pallas_call(functools.partial(rotation_kernel, total_rows), out_shape=...]
    ppermute x0 -> x21, waiting for transfers between devices: none -> 11.9 us  [send(): return lax.ppermute(value, AXES, device_permutation(move))]
    scatter x1 -> x0, local copies, waits for them, and re-layouts: 8.27 us -> none  [body(): restored = jnp.zeros_like(ordered).at[seating].set(ordered)]
  transfers between devices with their start and end apart: 2 -> 21, of which waited for: 2 -> 8; matrix products, arithmetic and copies ran while one was open for 0% -> 0% of each run, Pallas kernels for 0% -> 9%
where the time goes in v2:
time: 71.7 us; the launch traced here: 71.6 us
  starting transfers between devices  39.7 us (55%)
  Pallas kernels  16.6 us (23%)
  waiting for transfers between devices  11.9 us (17%)
  local copies, waits for them, and re-layouts  2.86 us (4%)
    ppermute x21, starting transfers between devices, send(): return lax.ppermute(value, AXES, device_permutation(move))  39.7 us
    ppermute x21, waiting for transfers between devices, send(): return lax.ppermute(value, AXES, device_permutation(move))  11.9 us
    pallas_call x1, Pallas kernels, steps(): pl.pallas_call(functools.partial(rotation_kernel, total_rows), out_shape=...  4.55 us
    pallas_call x1, Pallas kernels, steps(): pl.pallas_call(far_kernel, out_shape=jax.ShapeDtypeStruct(columns.shape,...  4.38 us
    pallas_call x3, Pallas kernels, apply(): pl.pallas_call(near_kernel, out_shape=(jax.ShapeDtypeStruct((256, rows_he...  3.24 us
    pallas_call x2, Pallas kernels, gram(): pl.pallas_call(functools.partial(gram_kernel, first_slot, whole), out_sha...  2.95 us
    unnamed x8, local copies, waits for them, and re-layouts  2.85 us
    pallas_call x1, Pallas kernels, steps(): pl.pallas_call(split_kernel, out_shape=(jax.ShapeDtypeStruct((768, rows_h...  1.46 us
  transfers between devices with their start and end apart: 21, of which 8 were waited for; matrix products, arithmetic and copies ran while one was open for 0% of the time, Pallas kernels for 9%

profile of v2, /device:TPU:1, one launch (start us, length us, event | category | flops | bytes accessed | tf_op | source)
XLA Modules:
  0.0 71.6 jit_solution(3212636230628797427)
XLA Ops:
  0.0 2.2 %copy-done = f32[2048,512]{1,0:T(8,128)S(1)} copy-done((f32[2048,512]{1,0:T(8,128)S(1)}, f32[2048,512]{1,0:T(8,128)}, u32[]{:S(2)}) %copy-start) | copy-done | bytes 4194328
  2.2 0.7 copy-done.2
  2.8 1.5 %gram_away.1 = f32[4,264,128]{2,1,0:T(8,128)S(1)} custom-call(s32[32]{0:T(128)S(1)} %copy-done.2, f32[2048,512]{1,0:T(8,128)S(1)} %copy-done), custom_call_target="tpu_custom_call" | custom-call | flops 536870912 | bytes 2097152 | tf_op jit(solution)/shard_map/gram_away/pallas_call | solution.py:297
  4.3 3.3 %collective-permute-start = (f32[4,264,128]{2,1,0:T(8,128)S(1)}, f32[4,264,128]{2,1,0:T(8,128)S(1)}, u32[]{:S(2)}, u32[]{:S(2)}) collective-permute-start(f32[4,264,128]{2,1,0:T(8,128)S(1)} %gram_away.1), channel_id=1, source_target_pairs={{0,32},{1,33},{2,34},{3,35},{4,36},{5,37},{6,38},{7,39},{8,40},{9,... | collective-permute-start | bytes 1622024 | tf_op jit(solution)/shard_map/ppermute | solution.py:37
  7.6 1.5 %gram_home.1 = (f32[264,128]{1,0:T(8,128)S(1)}, f32[264,128]{1,0:T(8,128)S(1)}, f32[264,128]{1,0:T(8,128)S(1)}, f32[264,128]{1,0:T(8,128)S(1)}) custom-call(s32[32]{0:T(128)S(1)} %copy-done.2, f32[2048,512]{1,0:T(8,128)S(1)} %copy-done), custom_call_target="tpu_custom_call" | custom-call | flops 536870912 | bytes 2097152 | tf_op jit(solution)/shard_map/gram_home/pallas_call | solution.py:297
  9.1 0.1 collective-permute-done
  9.2 0.1 fusion
  9.2 0.1 collective-permute-start.1
  9.3 1.9 %collective-permute-start.2 = (f32[264,128]{1,0:T(8,128)S(1)}, f32[264,128]{1,0:T(8,128)S(1)}, u32[]{:S(2)}, u32[]{:S(2)}) collective-permute-start(f32[264,128]{1,0:T(8,128)S(1)} %get-tuple-element.39), channel_id=1, source_target_pairs={{0,128},{1,129},{2,130},{3,131},{4,132},{5,133},{6,134},{7,135},{8... | collective-permute-start | bytes 405512 | tf_op jit(solution)/shard_map/ppermute | solution.py:37
  11.3 1.2 %collective-permute-start.3 = (f32[264,128]{1,0:T(8,128)S(1)}, f32[264,128]{1,0:T(8,128)S(1)}, u32[]{:S(2)}, u32[]{:S(2)}) collective-permute-start(f32[264,128]{1,0:T(8,128)S(1)} %get-tuple-element.40), channel_id=1, source_target_pairs={{0,192},{1,193},{2,194},{3,195},{4,196},{5,197},{6,198},{7,199},{8... | collective-permute-start | bytes 405512 | tf_op jit(solution)/shard_map/ppermute | solution.py:37
  12.4 1.5 %split.1 = (bf16[768,512]{1,0:T(8,128)(2,1)S(1)}, bf16[768,512]{1,0:T(8,128)(2,1)S(1)}, bf16[768,512]{1,0:T(8,128)(2,1)S(1)}, bf16[768,512]{1,0:T(8,128)(2,1)S(1...) custom-call(s32[32]{0:T(128)S(1)} %copy-done.3, ...), custom_call_target="tpu_custom_call" | custom-call | bytes 10485760 | tf_op jit(solution)/shard_map/split/pallas_call | solution.py:313
  13.9 2.2 %collective-permute-done.1 = f32[264,128]{1,0:T(8,128)S(1)} collective-permute-done((f32[264,128]{1,0:T(8,128)S(1)}, f32[264,128]{1,0:T(8,128)S(1)}, u32[]{:S(2)}, u32[]{:S(2)}) %collective-permute-start.1) | collective-permute-done | bytes 135200 | tf_op jit(solution)/shard_map/ppermute | solution.py:37
  16.1 0.0 collective-permute-done.2
  16.1 0.6 collective-permute-done.3
  16.7 0.1 add_add_fusion
  16.8 0.4 collective-permute-start.4
  17.2 1.3 %collective-permute-start.9 = (f32[128,128]{1,0:T(8,128)S(1)}, f32[128,128]{1,0:T(8,128)S(1)}, u32[]{:S(2)}, u32[]{:S(2)}) collective-permute-start(f32[128,128]{1,0:T(8,128)S(1)} %slice.23), channel_id=1, source_target_pairs={{0,1},{1,0},{2,3},{3,2},{4,5},{5,4},{6,7},{7,6},{8,9},{9,8},{10,11... | collective-permute-start | bytes 196616 | tf_op jit(solution)/shard_map/ppermute | solution.py:37
  18.5 1.5 %collective-permute-done.4 = f32[136,128]{1,0:T(8,128)S(1)} collective-permute-done((f32[136,128]{1,0:T(8,128)S(1)}, f32[136,128]{1,0:T(8,128)S(1)}, u32[]{:S(2)}, u32[]{:S(2)}) %collective-permute-start.4) | collective-permute-done | bytes 69664 | tf_op jit(solution)/shard_map/ppermute | solution.py:37
  20.0 3.1 %collective-permute-start.5 = (f32[136,128]{1,0:T(8,128)S(1)}, f32[136,128]{1,0:T(8,128)S(1)}, u32[]{:S(2)}, u32[]{:S(2)}) collective-permute-start(f32[136,128]{1,0:T(8,128)S(1)} %slice_add_fusion.1), channel_id=1, source_target_pairs={{0,24},{1,25},{2,26},{3,27},{4,28},{5,29},{6,30},{7,31},{8,16},{9,... | collective-permute-start | bytes 208904 | tf_op jit(solution)/shard_map/ppermute | solution.py:37
  23.2 0.0 collective-permute-done.9
  23.2 2.8 %collective-permute-start.10 = (f32[128,128]{1,0:T(8,128)S(1)}, f32[128,128]{1,0:T(8,128)S(1)}, u32[]{:S(2)}, u32[]{:S(2)}) collective-permute-start(f32[128,128]{1,0:T(8,128)S(1)} %slice_add_fusion), channel_id=1, source_target_pairs={{0,3},{1,2},{2,1},{3,0},{4,7},{5,6},{6,5},{7,4},{8,11},{9,10},{10,... | collective-permute-start | bytes 196616 | tf_op jit(solution)/shard_map/ppermute | solution.py:37
  26.0 0.0 collective-permute-done.5
  26.0 4.0 %collective-permute-start.6 = (f32[136,128]{1,0:T(8,128)S(1)}, f32[136,128]{1,0:T(8,128)S(1)}, u32[]{:S(2)}, u32[]{:S(2)}) collective-permute-start(f32[136,128]{1,0:T(8,128)S(1)} %add.59), channel_id=1, source_target_pairs={{0,1},{1,0},{2,3},{3,2},{4,5},{5,4},{6,7},{7,6},{8,9},{9,8},{10,11... | collective-permute-start | bytes 208904 | tf_op jit(solution)/shard_map/ppermute | solution.py:37
  30.0 0.1 collective-permute-start.11
  30.1 1.7 %collective-permute-done.6 = f32[136,128]{1,0:T(8,128)S(1)} collective-permute-done((f32[136,128]{1,0:T(8,128)S(1)}, f32[136,128]{1,0:T(8,128)S(1)}, u32[]{:S(2)}, u32[]{:S(2)}) %collective-permute-start.6) | collective-permute-done | bytes 69664 | tf_op jit(solution)/shard_map/ppermute | solution.py:37
  31.9 0.9 %collective-permute-start.7 = (f32[136,128]{1,0:T(8,128)S(1)}, f32[136,128]{1,0:T(8,128)S(1)}, u32[]{:S(2)}, u32[]{:S(2)}) collective-permute-start(f32[136,128]{1,0:T(8,128)S(1)} %add.60), channel_id=1, source_target_pairs={{0,3},{1,2},{2,1},{3,0},{4,7},{5,6},{6,5},{7,4},{8,11},{9,10},{10,... | collective-permute-start | bytes 208904 | tf_op jit(solution)/shard_map/ppermute | solution.py:37
  32.7 1.5 %collective-permute-done.11 = f32[128,128]{1,0:T(8,128)S(1)} collective-permute-done((f32[128,128]{1,0:T(8,128)S(1)}, f32[128,128]{1,0:T(8,128)S(1)}, u32[]{:S(2)}, u32[]{:S(2)}) %collective-permute-start.11) | collective-permute-done | bytes 65568 | tf_op jit(solution)/shard_map/ppermute | solution.py:37
  34.3 1.9 %collective-permute-start.12 = (f32[128,128]{1,0:T(8,128)S(1)}, f32[128,128]{1,0:T(8,128)S(1)}, u32[]{:S(2)}, u32[]{:S(2)}) collective-permute-start(f32[128,128]{1,0:T(8,128)S(1)} %add.65), channel_id=1, source_target_pairs={{0,8},{1,9},{2,10},{3,11},{4,12},{5,13},{6,14},{7,15},{8,0},{9,1},... | collective-permute-start | bytes 196616 | tf_op jit(solution)/shard_map/ppermute | solution.py:37
  36.2 2.4 %collective-permute-start.8 = (f32[136,128]{1,0:T(8,128)S(1)}, f32[136,128]{1,0:T(8,128)S(1)}, u32[]{:S(2)}, u32[]{:S(2)}) collective-permute-start(f32[136,128]{1,0:T(8,128)S(1)} %add.61), channel_id=1, source_target_pairs={{0,7},{1,6},{2,5},{3,4},{4,3},{5,2},{6,1},{7,0},{8,15},{9,14},{10,... | collective-permute-start | bytes 208904 | tf_op jit(solution)/shard_map/ppermute | solution.py:37
  38.5 1.2 %collective-permute-done.12 = f32[128,128]{1,0:T(8,128)S(1)} collective-permute-done((f32[128,128]{1,0:T(8,128)S(1)}, f32[128,128]{1,0:T(8,128)S(1)}, u32[]{:S(2)}, u32[]{:S(2)}) %collective-permute-start.12) | collective-permute-done | bytes 65568 | tf_op jit(solution)/shard_map/ppermute | solution.py:37
  39.7 1.4 %collective-permute-start.13 = (f32[128,128]{1,0:T(8,128)S(1)}, f32[128,128]{1,0:T(8,128)S(1)}, u32[]{:S(2)}, u32[]{:S(2)}) collective-permute-start(f32[128,128]{1,0:T(8,128)S(1)} %add.66), channel_id=1, source_target_pairs={{0,24},{1,25},{2,26},{3,27},{4,28},{5,29},{6,30},{7,31},{8,16},{9,... | collective-permute-start | bytes 196616 | tf_op jit(solution)/shard_map/ppermute | solution.py:37
  41.2 3.2 %collective-permute-done.13 = f32[128,128]{1,0:T(8,128)S(1)} collective-permute-done((f32[128,128]{1,0:T(8,128)S(1)}, f32[128,128]{1,0:T(8,128)S(1)}, u32[]{:S(2)}, u32[]{:S(2)}) %collective-permute-start.13) | collective-permute-done | bytes 65568 | tf_op jit(solution)/shard_map/ppermute | solution.py:37
  44.3 0.0 collective-permute-done.8
  44.3 4.5 %rotation.1.refs_0_ = f32[264,128]{1,0:T(8,128)S(1)} custom-call(f32[136,128]{1,0:T(8,128)S(1)} %add.62.straight, f32[128,128]{1,0:T(8,128)S(1)} %add.67.crossed), custom_call_target="tpu_custom_call" | custom-call | tf_op jit(solution)/shard_map/rotation/pallas_call | solution.py:329
  48.9 0.6 collective-permute-start.19
  49.5 1.3 %collective-permute-start.17 = (f32[264,128]{1,0:T(8,128)S(1)}, f32[264,128]{1,0:T(8,128)S(1)}, u32[]{:S(2)}, u32[]{:S(2)}) collective-permute-start(f32[264,128]{1,0:T(8,128)S(1)} %rotation.1.refs_0_), channel_id=1, source_target_pairs={{0,128},{1,129},{2,130},{3,131},{4,132},{5,133},{6,134},{7,135},{8... | collective-permute-start | bytes 405512 | tf_op jit(solution)/shard_map/ppermute | solution.py:37
  50.8 1.8 %collective-permute-start.15 = (f32[264,128]{1,0:T(8,128)S(1)}, f32[264,128]{1,0:T(8,128)S(1)}, u32[]{:S(2)}, u32[]{:S(2)}) collective-permute-start(f32[264,128]{1,0:T(8,128)S(1)} %rotation.1.refs_0_), channel_id=1, source_target_pairs={{0,192},{1,193},{2,194},{3,195},{4,196},{5,197},{6,198},{7,199},{8... | collective-permute-start | bytes 405512 | tf_op jit(solution)/shard_map/ppermute | solution.py:37
  52.6 7.3 %collective-permute-start.14 = (f32[264,128]{1,0:T(8,128)S(1)}, f32[264,128]{1,0:T(8,128)S(1)}, u32[]{:S(2)}, u32[]{:S(2)}) collective-permute-start(f32[264,128]{1,0:T(8,128)S(1)} %rotation.1.refs_0_), channel_id=1, source_target_pairs={{0,32},{1,33},{2,34},{3,35},{4,36},{5,37},{6,38},{7,39},{8,40},{9,... | collective-permute-start | bytes 405512 | tf_op jit(solution)/shard_map/ppermute | solution.py:37
  59.9 1.0 %collective-permute-start.20 = (f32[264,128]{1,0:T(8,128)S(1)}, f32[264,128]{1,0:T(8,128)S(1)}, u32[]{:S(2)}, u32[]{:S(2)}) collective-permute-start(f32[264,128]{1,0:T(8,128)S(1)} %collective-permute-done.19.refs_1_), channel_id=1, source_target_pairs={{0,32},{1,33},{2,34},{3,35},{4,36},{5,37},{6,38},{7,39},{8,40},{9,... | collective-permute-start | bytes 405512 | tf_op jit(solution)/shard_map/ppermute | solution.py:37
  60.8 2.3 %collective-permute-start.18 = (f32[264,128]{1,0:T(8,128)S(1)}, f32[264,128]{1,0:T(8,128)S(1)}, u32[]{:S(2)}, u32[]{:S(2)}) collective-permute-start(f32[264,128]{1,0:T(8,128)S(1)} %collective-permute-done.17.refs_0_), channel_id=1, source_target_pairs={{0,32},{1,33},{2,34},{3,35},{4,36},{5,37},{6,38},{7,39},{8,40},{9,... | collective-permute-start | bytes 405512 | tf_op jit(solution)/shard_map/ppermute | solution.py:37
  63.2 0.0 collective-permute-done.15.refs_0_
  63.2 0.6 collective-permute-start.16
  63.7 0.9 %apply_near.3.refs_8_ = f32[256,512]{1,0:T(8,128)S(1)} custom-call(f32[264,128]{1,0:T(8,128)S(1)} %rotation.1.refs_0_, bf16[768,512]{1,0:T(8,128)(2,1)S(1)} %get-tuple-element.55.refs_1_), custom_call_target="tpu_custom_call" | custom-call | flops 402653184 | bytes 1048576 | tf_op jit(solution)/shard_map/apply_near/pallas_call | solution.py:340
  64.6 0.9 %apply_near.4.refs_9_ = f32[256,512]{1,0:T(8,128)S(1)} custom-call(f32[264,128]{1,0:T(8,128)S(1)} %collective-permute-done.15.refs_0_, bf16[768,512]{1,0:T(8,128)(2,1)S(1)} %get-tuple-element.56.refs_1_), custom_call_target="tpu_custom_call" | custom-call | flops 402653184 | bytes 1048576 | tf_op jit(solution)/shard_map/apply_near/pallas_call | solution.py:340
  65.5 1.5 %apply_near.5 = (f32[256,512]{1,0:T(8,128)S(1)}, f32[256,512]{1,0:T(8,128)S(1)}) custom-call(f32[264,128]{1,0:T(8,128)S(1)} %collective-permute-done.17.refs_0_, f32[264,128]{1,0:T(8,128)S(1)} %collective-permute-done.19.refs_1_, bf16[768,512]{1,0:T(8,128)(2,1)S(1)} %get-tuple-element.57.refs_2_, bf16[768,512]{1,0:T(8,128)(2,1)S(1)} %get-tuple-element.58.refs_3_), custom_call_target="tpu_custom_call" | custom-call | flops 805306368 | bytes 2097152 | tf_op jit(solution)/shard_map/apply_near/pallas_call | solution.py:340
  67.0 0.0 collective-permute-done.14.refs_0_
  67.0 0.0 collective-permute-done.20.refs_3_
  67.0 4.4 %apply_far.1 = f32[2048,512]{1,0:T(8,128)} custom-call(s32[32]{0:T(128)S(1)} %copy-done.3, f32[264,128]{1,0:T(8,128)S(1)} %collective-permute-done.14.refs_0_, f32[264,128]{1,0:T(8,128)S(1)} %collective-permute-done.16.refs_1_, f32[264,128]{1,0:T(8,128)S(1)} %collective-permute-done.18.refs_2_, f32[264,128]{1,0:T(8,128)S(1)} %collective-permute-done.20.refs_3_, ...), custom_call_target="tpu_custom_call" | custom-call | tf_op jit(solution)/shard_map/apply_far/pallas_call | solution.py:359
  (24 shorter events, 0.1 us)
Async XLA Ops:
  0.0 2.2 %copy-start = (f32[2048,512]{1,0:T(8,128)S(1)}, f32[2048,512]{1,0:T(8,128)}, u32[]{:S(2)}) copy-start(f32[2048,512]{1,0:T(8,128)} %columns.5) | copy-start | bytes 12582916
  2.2 0.7 copy-start.2
  2.8 9.6 %copy-start.1 = (f32[2048,512]{1,0:T(8,128)S(1)}, f32[2048,512]{1,0:T(8,128)}, u32[]{:S(2)}) copy-start(f32[2048,512]{1,0:T(8,128)} %columns.5) | copy-start | bytes 12582916
  2.8 9.6 %copy-start.3 = (s32[32]{0:T(128)S(1)}, s32[32]{0:T(128)}, u32[]{:S(2)}) copy-start(s32[32]{0:T(128)} %seating.6) | copy-start | bytes 388
  4.3 4.8 %collective-permute-start = (f32[4,264,128]{2,1,0:T(8,128)S(1)}, f32[4,264,128]{2,1,0:T(8,128)S(1)}, u32[]{:S(2)}, u32[]{:S(2)}) collective-permute-start(f32[4,264,128]{2,1,0:T(8,128)S(1)} %gram_away.1), channel_id=1, source_target_pairs={{0,32},{1,33},{2,34},{3,35},{4,36},{5,37},{6,38},{7,39},{8,40},{9,... | collective-permute-start | bytes 1622024 | tf_op jit(solution)/shard_map/ppermute | solution.py:37
  9.2 6.9 %collective-permute-start.1 = (f32[264,128]{1,0:T(8,128)S(1)}, f32[264,128]{1,0:T(8,128)S(1)}, u32[]{:S(2)}, u32[]{:S(2)}) collective-permute-start(f32[264,128]{1,0:T(8,128)S(1)} %get-tuple-element.38), channel_id=1, source_target_pairs={{0,64},{1,65},{2,66},{3,67},{4,68},{5,69},{6,70},{7,71},{8,72},{9,... | collective-permute-start | bytes 405512 | tf_op jit(solution)/shard_map/ppermute | solution.py:37
  9.3 6.8 %collective-permute-start.2 = (f32[264,128]{1,0:T(8,128)S(1)}, f32[264,128]{1,0:T(8,128)S(1)}, u32[]{:S(2)}, u32[]{:S(2)}) collective-permute-start(f32[264,128]{1,0:T(8,128)S(1)} %get-tuple-element.39), channel_id=1, source_target_pairs={{0,128},{1,129},{2,130},{3,131},{4,132},{5,133},{6,134},{7,135},{8... | collective-permute-start | bytes 405512 | tf_op jit(solution)/shard_map/ppermute | solution.py:37
  11.3 5.4 %collective-permute-start.3 = (f32[264,128]{1,0:T(8,128)S(1)}, f32[264,128]{1,0:T(8,128)S(1)}, u32[]{:S(2)}, u32[]{:S(2)}) collective-permute-start(f32[264,128]{1,0:T(8,128)S(1)} %get-tuple-element.40), channel_id=1, source_target_pairs={{0,192},{1,193},{2,194},{3,195},{4,196},{5,197},{6,198},{7,199},{8... | collective-permute-start | bytes 405512 | tf_op jit(solution)/shard_map/ppermute | solution.py:37
  16.8 3.2 %collective-permute-start.4 = (f32[136,128]{1,0:T(8,128)S(1)}, f32[136,128]{1,0:T(8,128)S(1)}, u32[]{:S(2)}, u32[]{:S(2)}) collective-permute-start(f32[136,128]{1,0:T(8,128)S(1)} %slice.22), channel_id=1, source_target_pairs={{0,8},{1,9},{2,10},{3,11},{4,12},{5,13},{6,14},{7,15},{8,0},{9,1},... | collective-permute-start | bytes 208904 | tf_op jit(solution)/shard_map/ppermute | solution.py:37
  17.2 6.0 %collective-permute-start.9 = (f32[128,128]{1,0:T(8,128)S(1)}, f32[128,128]{1,0:T(8,128)S(1)}, u32[]{:S(2)}, u32[]{:S(2)}) collective-permute-start(f32[128,128]{1,0:T(8,128)S(1)} %slice.23), channel_id=1, source_target_pairs={{0,1},{1,0},{2,3},{3,2},{4,5},{5,4},{6,7},{7,6},{8,9},{9,8},{10,11... | collective-permute-start | bytes 196616 | tf_op jit(solution)/shard_map/ppermute | solution.py:37
  20.0 6.0 %collective-permute-start.5 = (f32[136,128]{1,0:T(8,128)S(1)}, f32[136,128]{1,0:T(8,128)S(1)}, u32[]{:S(2)}, u32[]{:S(2)}) collective-permute-start(f32[136,128]{1,0:T(8,128)S(1)} %slice_add_fusion.1), channel_id=1, source_target_pairs={{0,24},{1,25},{2,26},{3,27},{4,28},{5,29},{6,30},{7,31},{8,16},{9,... | collective-permute-start | bytes 208904 | tf_op jit(solution)/shard_map/ppermute | solution.py:37
  23.2 6.8 %collective-permute-start.10 = (f32[128,128]{1,0:T(8,128)S(1)}, f32[128,128]{1,0:T(8,128)S(1)}, u32[]{:S(2)}, u32[]{:S(2)}) collective-permute-start(f32[128,128]{1,0:T(8,128)S(1)} %slice_add_fusion), channel_id=1, source_target_pairs={{0,3},{1,2},{2,1},{3,0},{4,7},{5,6},{6,5},{7,4},{8,11},{9,10},{10,... | collective-permute-start | bytes 196616 | tf_op jit(solution)/shard_map/ppermute | solution.py:37
  26.0 5.8 %collective-permute-start.6 = (f32[136,128]{1,0:T(8,128)S(1)}, f32[136,128]{1,0:T(8,128)S(1)}, u32[]{:S(2)}, u32[]{:S(2)}) collective-permute-start(f32[136,128]{1,0:T(8,128)S(1)} %add.59), channel_id=1, source_target_pairs={{0,1},{1,0},{2,3},{3,2},{4,5},{5,4},{6,7},{7,6},{8,9},{9,8},{10,11... | collective-permute-start | bytes 208904 | tf_op jit(solution)/shard_map/ppermute | solution.py:37
  30.0 4.2 %collective-permute-start.11 = (f32[128,128]{1,0:T(8,128)S(1)}, f32[128,128]{1,0:T(8,128)S(1)}, u32[]{:S(2)}, u32[]{:S(2)}) collective-permute-start(f32[128,128]{1,0:T(8,128)S(1)} %add.64), channel_id=1, source_target_pairs={{0,7},{1,6},{2,5},{3,4},{4,3},{5,2},{6,1},{7,0},{8,15},{9,14},{10,... | collective-permute-start | bytes 196616 | tf_op jit(solution)/shard_map/ppermute | solution.py:37
  31.9 4.3 %collective-permute-start.7 = (f32[136,128]{1,0:T(8,128)S(1)}, f32[136,128]{1,0:T(8,128)S(1)}, u32[]{:S(2)}, u32[]{:S(2)}) collective-permute-start(f32[136,128]{1,0:T(8,128)S(1)} %add.60), channel_id=1, source_target_pairs={{0,3},{1,2},{2,1},{3,0},{4,7},{5,6},{6,5},{7,4},{8,11},{9,10},{10,... | collective-permute-start | bytes 208904 | tf_op jit(solution)/shard_map/ppermute | solution.py:37
  34.3 5.4 %collective-permute-start.12 = (f32[128,128]{1,0:T(8,128)S(1)}, f32[128,128]{1,0:T(8,128)S(1)}, u32[]{:S(2)}, u32[]{:S(2)}) collective-permute-start(f32[128,128]{1,0:T(8,128)S(1)} %add.65), channel_id=1, source_target_pairs={{0,8},{1,9},{2,10},{3,11},{4,12},{5,13},{6,14},{7,15},{8,0},{9,1},... | collective-permute-start | bytes 196616 | tf_op jit(solution)/shard_map/ppermute | solution.py:37
  36.2 8.1 %collective-permute-start.8 = (f32[136,128]{1,0:T(8,128)S(1)}, f32[136,128]{1,0:T(8,128)S(1)}, u32[]{:S(2)}, u32[]{:S(2)}) collective-permute-start(f32[136,128]{1,0:T(8,128)S(1)} %add.61), channel_id=1, source_target_pairs={{0,7},{1,6},{2,5},{3,4},{4,3},{5,2},{6,1},{7,0},{8,15},{9,14},{10,... | collective-permute-start | bytes 208904 | tf_op jit(solution)/shard_map/ppermute | solution.py:37
  39.7 4.6 %collective-permute-start.13 = (f32[128,128]{1,0:T(8,128)S(1)}, f32[128,128]{1,0:T(8,128)S(1)}, u32[]{:S(2)}, u32[]{:S(2)}) collective-permute-start(f32[128,128]{1,0:T(8,128)S(1)} %add.66), channel_id=1, source_target_pairs={{0,24},{1,25},{2,26},{3,27},{4,28},{5,29},{6,30},{7,31},{8,16},{9,... | collective-permute-start | bytes 196616 | tf_op jit(solution)/shard_map/ppermute | solution.py:37
  48.9 11.0 %collective-permute-start.19 = (f32[264,128]{1,0:T(8,128)S(1)}, f32[264,128]{1,0:T(8,128)S(1)}, u32[]{:S(2)}, u32[]{:S(2)}) collective-permute-start(f32[264,128]{1,0:T(8,128)S(1)} %rotation.1.refs_0_), channel_id=1, source_target_pairs={{0,64},{1,65},{2,66},{3,67},{4,68},{5,69},{6,70},{7,71},{8,72},{9,... | collective-permute-start | bytes 405512 | tf_op jit(solution)/shard_map/ppermute | solution.py:37
  49.5 11.3 %collective-permute-start.17 = (f32[264,128]{1,0:T(8,128)S(1)}, f32[264,128]{1,0:T(8,128)S(1)}, u32[]{:S(2)}, u32[]{:S(2)}) collective-permute-start(f32[264,128]{1,0:T(8,128)S(1)} %rotation.1.refs_0_), channel_id=1, source_target_pairs={{0,128},{1,129},{2,130},{3,131},{4,132},{5,133},{6,134},{7,135},{8... | collective-permute-start | bytes 405512 | tf_op jit(solution)/shard_map/ppermute | solution.py:37
  50.8 12.3 %collective-permute-start.15 = (f32[264,128]{1,0:T(8,128)S(1)}, f32[264,128]{1,0:T(8,128)S(1)}, u32[]{:S(2)}, u32[]{:S(2)}) collective-permute-start(f32[264,128]{1,0:T(8,128)S(1)} %rotation.1.refs_0_), channel_id=1, source_target_pairs={{0,192},{1,193},{2,194},{3,195},{4,196},{5,197},{6,198},{7,199},{8... | collective-permute-start | bytes 405512 | tf_op jit(solution)/shard_map/ppermute | solution.py:37
  52.6 14.4 %collective-permute-start.14 = (f32[264,128]{1,0:T(8,128)S(1)}, f32[264,128]{1,0:T(8,128)S(1)}, u32[]{:S(2)}, u32[]{:S(2)}) collective-permute-start(f32[264,128]{1,0:T(8,128)S(1)} %rotation.1.refs_0_), channel_id=1, source_target_pairs={{0,32},{1,33},{2,34},{3,35},{4,36},{5,37},{6,38},{7,39},{8,40},{9,... | collective-permute-start | bytes 405512 | tf_op jit(solution)/shard_map/ppermute | solution.py:37
  59.9 7.2 %collective-permute-start.20 = (f32[264,128]{1,0:T(8,128)S(1)}, f32[264,128]{1,0:T(8,128)S(1)}, u32[]{:S(2)}, u32[]{:S(2)}) collective-permute-start(f32[264,128]{1,0:T(8,128)S(1)} %collective-permute-done.19.refs_1_), channel_id=1, source_target_pairs={{0,32},{1,33},{2,34},{3,35},{4,36},{5,37},{6,38},{7,39},{8,40},{9,... | collective-permute-start | bytes 405512 | tf_op jit(solution)/shard_map/ppermute | solution.py:37
  60.8 6.2 %collective-permute-start.18 = (f32[264,128]{1,0:T(8,128)S(1)}, f32[264,128]{1,0:T(8,128)S(1)}, u32[]{:S(2)}, u32[]{:S(2)}) collective-permute-start(f32[264,128]{1,0:T(8,128)S(1)} %collective-permute-done.17.refs_0_), channel_id=1, source_target_pairs={{0,32},{1,33},{2,34},{3,35},{4,36},{5,37},{6,38},{7,39},{8,40},{9,... | collective-permute-start | bytes 405512 | tf_op jit(solution)/shard_map/ppermute | solution.py:37
  63.2 3.9 %collective-permute-start.16 = (f32[264,128]{1,0:T(8,128)S(1)}, f32[264,128]{1,0:T(8,128)S(1)}, u32[]{:S(2)}, u32[]{:S(2)}) collective-permute-start(f32[264,128]{1,0:T(8,128)S(1)} %collective-permute-done.15.refs_0_), channel_id=1, source_target_pairs={{0,32},{1,33},{2,34},{3,35},{4,36},{5,37},{6,38},{7,39},{8,40},{9,... | collective-permute-start | bytes 405512 | tf_op jit(solution)/shard_map/ppermute | solution.py:37

commit v3 on v2

--- a/solution.py
+++ b/solution.py
@@ -15,9 +15,8 @@
 SPREAD = 4
 CHUNK = 264
 CUT = 136
+FAR_FIRST = (2, 1, 3, 0)
 MIB = 1 << 20
-GRAM_MIB = 8
-SPLIT_MIB = 8
 
 
 def device_permutation(move):
@@ -61,13 +60,9 @@
     return lambda y, c, x, z: first(y, c, x, z) if c == 0 else second(y, c, x, z)
 
 
-EXCHANGES = tuple(
-    by_core(first, second)
-    for first, second in (
-        *zip(pairings("x") + pairings("z"), pairings("z") + pairings("y")),
-        *zip(pairings("z") + pairings("x"), pairings("y") + pairings("z")),
-    )
-)
+EXCHANGES = tuple(by_core(first, second) for first, second in zip(pairings("z") + pairings("x"), pairings("z") + pairings("y")))
+EVEN_ORDER = (0, 1, 2, 3, 4)
+ODD_ORDER = (3, 4, 0, 1, 2)
 
 
 def group_at(slot):
@@ -138,22 +133,47 @@
     return dot_t(left, jnp.concatenate([high, middle, high, middle, low, high], axis=1))
 
 
-def gram_kernel(first_slot, whole, seating, columns, *outs):
-    for k in range(SPREAD):
-        seats = blocks_of(first_slot + k)
-        value = jnp.concatenate([columns[seat_rows(seating, seat), :] for seat in seats], axis=0)
-        high = value.astype(jnp.bfloat16)
-        low = (value - high.astype(jnp.float32)).astype(jnp.bfloat16)
-        both = dot_t(jnp.concatenate([high, low], axis=0), high)
-        even, odd = both[:256], both[256:]
-        upper = even[:128, :128] + odd[:128, :128] + odd[:128, :128].T
-        cross = even[:128, 128:] + odd[:128, 128:] + odd[128:, :128].T
-        lower = even[128:, 128:] + odd[128:, 128:] + odd[128:, 128:].T
-        folded, diagonal = fold(upper, lower)
-        out = outs[0].at[k] if whole else outs[k]
-        out[0:128, :] = folded
-        out[128:136, :] = jnp.broadcast_to(diagonal, (8, 128))
-        out[136:264, :] = cross
+def away_kernel(seating, columns, *refs):
+    outs, (panel, sems) = refs[:-2], refs[-2:]
+    copies = [
+        [
+            pltpu.make_async_copy(
+                columns.at[seat_rows(seating, seat), :], panel.at[slot, pl.ds(n * BLOCK, BLOCK), :], sems.at[slot, n]
+            )
+            for n, seat in enumerate(blocks_of(slot))
+        ]
+        for slot in range(2 * SPREAD)
+    ]
+    for group in copies:
+        for copy in group:
+            copy.start()
+    for group in copies[:SPREAD]:
+        for copy in group:
+            copy.wait()
+    for k, out in enumerate(outs):
+        folded_gram(panel[k], out)
+    for group in copies[SPREAD:]:
+        for copy in group:
+            copy.wait()
+
+
+def home_kernel(panel, *outs):
+    for k, out in enumerate(outs):
+        folded_gram(panel[SPREAD + k], out)
+
+
+def folded_gram(value, out):
+    high = value.astype(jnp.bfloat16)
+    low = (value - high.astype(jnp.float32)).astype(jnp.bfloat16)
+    both = dot_t(jnp.concatenate([high, low], axis=0), high)
+    even, odd = both[:256], both[256:]
+    upper = even[:128, :128] + odd[:128, :128] + odd[:128, :128].T
+    cross = even[:128, 128:] + odd[:128, 128:] + odd[128:, :128].T
+    lower = even[128:, 128:] + odd[128:, 128:] + odd[128:, 128:].T
+    folded, diagonal = fold(upper, lower)
+    out[0:128, :] = folded
+    out[128:136, :] = jnp.broadcast_to(diagonal, (8, 128))
+    out[136:264, :] = cross
 
 
 def rotations(grams, total_rows):
@@ -194,10 +214,17 @@
     )
 
 
-def rotation_kernel(total_rows, straight, crossed, out):
+def even_kernel(total_rows, straight, out):
     first, second = unfold(straight[0:128], straight[128:129])
+    va, vb = rotations([first, second], total_rows)
+    out[0:128], diagonal = fold(va, vb)
+    out[128:136] = jnp.broadcast_to(diagonal, (8, 128))
+
+
+def odd_kernel(total_rows, straight, turned_even, crossed, out):
+    first, second = unfold(straight[0:128], straight[128:129])
+    va, vb = unfold(turned_even[0:128], turned_even[128:129])
     cross = crossed[...]
-    va, vb = rotations([first, second], total_rows)
     pa, pb = pieces(va), pieces(vb)
     top = mm(pa, pieces(jnp.concatenate([first, cross], axis=1)))
     bottom = mm(pb, pieces(jnp.concatenate([cross.T, second], axis=1)))
@@ -208,19 +235,16 @@
         right = tuple(stack_rows(p, q, half) for p, q in zip(pa, pb))
         grams.append(mm_t(left, right))
     vc, vd = rotations(grams, total_rows)
-    ab, b_diagonal = fold(va, vb)
-    cd, d_diagonal = fold(vc, vd)
-    out[0:128] = ab
-    out[128:256] = cd
+    out[0:128] = turned_even[0:128]
+    out[128:256], d_diagonal = fold(vc, vd)
     i, _ = indices((8, 128))
-    out[256:264] = jnp.where(i == 0, b_diagonal, d_diagonal)
-
-
-def split_kernel(seating, columns, *outs):
+    out[256:264] = jnp.where(i == 0, turned_even[128:136], d_diagonal)
+
+
+def split_kernel(panel, *outs):
     for slot in range(2 * SPREAD):
-        for n, seat in enumerate(blocks_of(slot)):
-            for part, value in enumerate(pieces(columns[seat_rows(seating, seat), :])):
-                outs[slot][pl.ds(part * 256 + n * BLOCK, BLOCK), :] = value
+        for part, value in enumerate(pieces(panel[slot])):
+            outs[slot][pl.ds(part * 256, 256), :] = value
 
 
 def turned(turn, panel):
@@ -244,27 +268,32 @@
         out[...] = turned(turn[...], panel[...])
 
 
-def far_kernel(seating, *refs):
-    turns, panels, done = refs[:SPREAD], refs[SPREAD : 2 * SPREAD], refs[2 * SPREAD : 3 * SPREAD]
-    out, result, sems = refs[3 * SPREAD :]
+def far_kernel(last, early, seating, *refs):
+    count = len(last)
+    turns, panels, done = refs[:count], refs[count : 2 * count], refs[2 * count : -5]
+    out, result, order, sems, order_sem = refs[-5:]
+    fetch = pltpu.make_async_copy(seating, order, order_sem)
+    fetch.start()
 
     def stores(slot, value):
         group = group_at(slot)
         return [
             pltpu.make_async_copy(
-                value.at[pl.ds(n * BLOCK, BLOCK), :], out.at[seat_rows(seating, seat), :], sems.at[slot, n]
+                value.at[pl.ds(n * BLOCK, BLOCK), :], out.at[seat_rows(order, seat), :], sems.at[slot, n]
             )
             for n, seat in enumerate((2 * group, 2 * group + 16, 2 * group + 1, 2 * group + 17))
         ]
 
     copies = []
-    for k in range(SPREAD):
-        copies += stores(SPREAD + k, done[k])
-    for copy in copies:
-        copy.start()
-    for k in range(SPREAD):
+    for k, slot in enumerate(last):
         result[k] = turned(turns[k][...], panels[k][...])
-        for copy in stores(k, result.at[k]):
+        if k == 0:
+            fetch.wait()
+            for waiting, value in zip(early, done):
+                copies += stores(waiting, value)
+            for copy in copies:
+                copy.start()
+        for copy in stores(slot, result.at[k]):
             copy.start()
             copies.append(copy)
     for copy in copies:
@@ -278,13 +307,14 @@
 
 
 def steps(columns, seating):
+    columns = pltpu.with_memory_space_constraint(columns, pltpu.MemorySpace.HBM)
+    seating = pltpu.with_memory_space_constraint(seating, pltpu.MemorySpace.HBM)
     rows_here = columns.shape[1]
     total_rows = float(rows_here * lax.axis_size(AXES))
     smem = pl.BlockSpec(memory_space=pltpu.SMEM)
     hbm = pl.BlockSpec(memory_space=pltpu.MemorySpace.HBM)
     vmem = pl.BlockSpec(memory_space=pltpu.VMEM)
     chunk = jax.ShapeDtypeStruct((CHUNK, 128), jnp.float32)
-    quarter = jax.ShapeDtypeStruct((SPREAD, CHUNK, 128), jnp.float32)
     panel_flops = 2 * 256 * 256 * rows_here
 
     def params(mib):
@@ -293,47 +323,66 @@
     def cost(flops, moved):
         return pl.CostEstimate(flops=flops, bytes_accessed=moved, transcendentals=0)
 
-    def gram(first_slot, whole):
-        return pl.pallas_call(
-            functools.partial(gram_kernel, first_slot, whole),
-            out_shape=quarter if whole else (chunk,) * SPREAD,
-            in_specs=[smem, vmem],
-            out_specs=vmem if whole else (vmem,) * SPREAD,
-            compiler_params=params(GRAM_MIB),
-            cost_estimate=cost(2 * SPREAD * panel_flops, 2 * MIB),
-            name="gram_away" if whole else "gram_home",
-        )(seating, columns)
-
-    away = gram(0, True)
-    passed = send(away, swap_core)
-    home = gram(SPREAD, False)
-    here = [home[d] + passed[d] for d in range(SPREAD)]
-
-    later, here = lax.optimization_barrier((seating, here))
+    *away, panel = pl.pallas_call(
+        away_kernel,
+        out_shape=(*(chunk,) * SPREAD, jax.ShapeDtypeStruct((2 * SPREAD, 256, rows_here), jnp.float32)),
+        in_specs=[smem, hbm],
+        out_specs=(vmem,) * (SPREAD + 1),
+        scratch_shapes=[pltpu.SemaphoreType.DMA((2 * SPREAD, 4))],
+        compiler_params=params(8),
+        name="gram_away",
+    )(seating, columns)
+    passed = {}
+    for d in FAR_FIRST:
+        passed[d] = send(away[d], swap_core)
+    home = pl.pallas_call(
+        home_kernel,
+        out_shape=(chunk,) * SPREAD,
+        in_specs=[vmem],
+        out_specs=(vmem,) * SPREAD,
+        compiler_params=params(8),
+        cost_estimate=cost(2 * SPREAD * panel_flops, 2 * MIB),
+        name="gram_home",
+    )(panel)
+    here = []
+    for d in range(SPREAD):
+        here.append(home[d] + passed[d])
+
+    panel, here[2] = lax.optimization_barrier((panel, here[2]))
     panels = pl.pallas_call(
         split_kernel,
         out_shape=(jax.ShapeDtypeStruct((768, rows_here), jnp.bfloat16),) * (2 * SPREAD),
-        in_specs=[smem, vmem],
+        in_specs=[vmem],
         out_specs=(vmem,) * (2 * SPREAD),
-        compiler_params=params(SPLIT_MIB),
+        compiler_params=params(8),
         cost_estimate=cost(0, 10 * MIB),
         name="split",
-    )(later, columns)
+    )(panel)
     arrived = []
     for d in range(1, SPREAD):
         arrived.append(send(here[d], shift(d)))
     total = here[0] + arrived[0] + arrived[1] + arrived[2]
     total, panels = lax.optimization_barrier((total, panels))
 
-    halves = [exchange(total[:CUT], (0, 1, 2, 3, 4)), exchange(total[CUT:], (5, 6, 7, 8, 9))]
-    turn = pl.pallas_call(
-        functools.partial(rotation_kernel, total_rows),
-        out_shape=chunk,
-        in_specs=[vmem, vmem],
+    straight = exchange(total[:CUT], EVEN_ORDER)
+    crossed = exchange(total[CUT:], ODD_ORDER)
+    even = pl.pallas_call(
+        functools.partial(even_kernel, total_rows),
+        out_shape=jax.ShapeDtypeStruct((CUT, 128), jnp.float32),
+        in_specs=[vmem],
         out_specs=vmem,
         compiler_params=params(8),
-        name="rotation",
-    )(*halves)
+        cost_estimate=cost(300 * 128**3, MIB),
+        name="rotation_even",
+    )(straight)
+    turn = pl.pallas_call(
+        functools.partial(odd_kernel, total_rows),
+        out_shape=chunk,
+        in_specs=[vmem] * 3,
+        out_specs=vmem,
+        compiler_params=params(8),
+        name="rotation_odd",
+    )(straight, even, crossed)
 
     def apply(slots, turns):
         count = len(slots)
@@ -353,21 +402,26 @@
     far = []
     for d in range(SPREAD):
         far.append(send(near[d], swap_core))
-    done = apply((4,), near[:1])
-    done += apply((5,), near[1:2])
-    done += apply((6, 7), near[2:])
+    early = []
+    for slots, turns in (
+        ((4,), near[:1]), ((0,), far[:1]), ((5,), near[1:2]), ((7, 6), [near[3], near[2]])
+    ):
+        early += [(slot, value) for slot, value in zip(slots, apply(slots, turns))]
+    last = (1, 3, 2)
     return pl.pallas_call(
-        far_kernel,
+        functools.partial(far_kernel, last, tuple(slot for slot, _ in early)),
         out_shape=jax.ShapeDtypeStruct(columns.shape, columns.dtype),
-        in_specs=[smem] + [vmem] * (3 * SPREAD),
+        in_specs=[hbm] + [vmem] * (2 * len(last) + len(early)),
         out_specs=hbm,
         scratch_shapes=[
-            pltpu.VMEM((SPREAD, 256, rows_here), jnp.float32),
+            pltpu.VMEM((len(last), 256, rows_here), jnp.float32),
+            pltpu.SMEM(seating.shape, seating.dtype),
             pltpu.SemaphoreType.DMA((2 * SPREAD, 4)),
+            pltpu.SemaphoreType.DMA,
         ],
         compiler_params=params(10),
         name="apply_far",
-    )(seating, *far, *[panels[slot] for slot in range(SPREAD)], *done)
+    )(seating, *[far[slot] for slot in last], *[panels[slot] for slot in last], *[value for _, value in early])
 
 
 def solution(mesh):

time: 71.7 us -> 71.9 us (level)
  starting transfers between devices: 39.7 us -> 43.4 us
  local copies, waits for them, and re-layouts: 2.86 us -> 0.01 us
  waiting for transfers between devices: 11.9 us -> 9.31 us
  Pallas kernels: 16.6 us -> 18.5 us
    ppermute x21 -> x24, starting transfers between devices: 39.7 us -> 43.4 us  [send(): return lax.ppermute(value, AXES, device_permutation(move))]
    unnamed x8 -> x0, local copies, waits for them, and re-layouts: 2.85 us -> none
    ppermute x21 -> x24, waiting for transfers between devices: 11.9 us -> 9.31 us  [send(): return lax.ppermute(value, AXES, device_permutation(move))]
    pallas_call x4 -> x5, Pallas kernels: 11.9 us -> 13.3 us  [the longest x1 4.17 us: steps(): pl.pallas_call(functools.partial(far_kernel, last, tuple((slot for slot,...]
    pallas_call x3 -> x4, Pallas kernels: 3.24 us -> 4.06 us  [apply(): pl.pallas_call(near_kernel, out_shape=(jax.ShapeDtypeStruct((256, rows_he...]
  transfers between devices with their start and end apart: 21 -> 24, of which waited for: 8 -> 8; matrix products, arithmetic and copies ran while one was open for 0% -> 0% of each run, Pallas kernels for 9% -> 9%
where the time goes in v3:
time: 71.9 us; the launch traced here: 71.8 us
  starting transfers between devices  43.4 us (60%)
  Pallas kernels  18.5 us (26%)
  waiting for transfers between devices  9.31 us (13%)
    ppermute x24, starting transfers between devices, send(): return lax.ppermute(value, AXES, device_permutation(move))  43.4 us
    ppermute x24, waiting for transfers between devices, send(): return lax.ppermute(value, AXES, device_permutation(move))  9.31 us
    pallas_call x1, Pallas kernels, steps(): pl.pallas_call(functools.partial(far_kernel, last, tuple((slot for slot,...  4.17 us
    pallas_call x4, Pallas kernels, apply(): pl.pallas_call(near_kernel, out_shape=(jax.ShapeDtypeStruct((256, rows_he...  4.06 us
    pallas_call x1, Pallas kernels, steps(): pl.pallas_call(away_kernel, out_shape=(*(chunk,) * SPREAD, jax.ShapeDtype...  3.47 us
    pallas_call x1, Pallas kernels, steps(): pl.pallas_call(functools.partial(odd_kernel, total_rows), out_shape=chunk...  2.67 us
    pallas_call x1, Pallas kernels, steps(): pl.pallas_call(functools.partial(even_kernel, total_rows), out_shape=jax....  2.09 us
  transfers between devices with their start and end apart: 24, of which 8 were waited for; matrix products, arithmetic and copies ran while one was open for 0% of the time, Pallas kernels for 9%

profile of v3, /device:TPU:1, one launch (start us, length us, event | category | flops | bytes accessed | tf_op | source)
XLA Modules:
  0.0 71.8 jit_solution(2096296432902215388)
XLA Ops:
  0.0 3.5 %gram_away.1 = (f32[264,128]{1,0:T(8,128)S(1)}, f32[264,128]{1,0:T(8,128)S(1)}, f32[264,128]{1,0:T(8,128)S(1)}, f32[264,128]{1,0:T(8,128)S(1)}, f32[8,256,512]{2,1,0:T(8,128)S(1)}) custom-call(s32[32]{0:T(128)} %seating.3, f32[2048,512]{1,0:T(8,128)} %columns.1), custom_call_target="tpu_custom_call" | custom-call | tf_op jit(solution)/shard_map/gram_away/pallas_call | solution.py:326
  3.5 3.3 %collective-permute-start.3 = (f32[264,128]{1,0:T(8,128)S(1)}, f32[264,128]{1,0:T(8,128)S(1)}, u32[]{:S(2)}, u32[]{:S(2)}) collective-permute-start(f32[264,128]{1,0:T(8,128)S(1)} %get-tuple-element.41), channel_id=1, source_target_pairs={{0,32},{1,33},{2,34},{3,35},{4,36},{5,37},{6,38},{7,39},{8,40},{9,... | collective-permute-start | bytes 405512 | tf_op jit(solution)/shard_map/ppermute | solution.py:36
  6.8 0.1 collective-permute-start.1
  6.9 0.4 collective-permute-start.5
  7.3 0.1 collective-permute-start
  7.4 0.9 %gram_home.1 = (f32[264,128]{1,0:T(8,128)S(1)}, f32[264,128]{1,0:T(8,128)S(1)}, f32[264,128]{1,0:T(8,128)S(1)}, f32[264,128]{1,0:T(8,128)S(1)}) custom-call(f32[8,256,512]{2,1,0:T(8,128)S(1)} %get-tuple-element.45.panel), custom_call_target="tpu_custom_call" | custom-call | flops 536870912 | bytes 2097152 | tf_op jit(solution)/shard_map/gram_home/pallas_call | solution.py:338
  8.3 1.1 %collective-permute-start.4 = (f32[264,128]{1,0:T(8,128)S(1)}, f32[264,128]{1,0:T(8,128)S(1)}, u32[]{:S(2)}, u32[]{:S(2)}) collective-permute-start(f32[264,128]{1,0:T(8,128)S(1)} %add.54), channel_id=1, source_target_pairs={{0,128},{1,129},{2,130},{3,131},{4,132},{5,133},{6,134},{7,135},{8... | collective-permute-start | bytes 405512 | tf_op jit(solution)/shard_map/ppermute | solution.py:36
  9.4 0.0 collective-permute-done.1
  9.4 0.4 collective-permute-start.2
  9.8 0.0 collective-permute-done.5
  9.8 2.4 %collective-permute-start.6 = (f32[264,128]{1,0:T(8,128)S(1)}, f32[264,128]{1,0:T(8,128)S(1)}, u32[]{:S(2)}, u32[]{:S(2)}) collective-permute-start(f32[264,128]{1,0:T(8,128)S(1)} %add.56), channel_id=1, source_target_pairs={{0,192},{1,193},{2,194},{3,195},{4,196},{5,197},{6,198},{7,199},{8... | collective-permute-start | bytes 405512 | tf_op jit(solution)/shard_map/ppermute | solution.py:36
  12.3 1.2 %split.1 = (bf16[768,512]{1,0:T(8,128)(2,1)S(1)}, bf16[768,512]{1,0:T(8,128)(2,1)S(1)}, bf16[768,512]{1,0:T(8,128)(2,1)S(1)}, bf16[768,512]{1,0:T(8,128)(2,1)S(1...) custom-call(f32[8,256,512]{2,1,0:T(8,128)S(1)} %get-tuple-element.45, ...), custom_call_target="tpu_custom_call" | custom-call | bytes 10485760 | tf_op jit(solution)/shard_map/split/pallas_call | solution.py:352
  13.5 0.0 collective-permute-done
  13.5 0.5 collective-permute-done.4
  14.0 1.4 %collective-permute-done.2 = f32[264,128]{1,0:T(8,128)S(1)} collective-permute-done((f32[264,128]{1,0:T(8,128)S(1)}, f32[264,128]{1,0:T(8,128)S(1)}, u32[]{:S(2)}, u32[]{:S(2)}) %collective-permute-start.2) | collective-permute-done | bytes 135200 | tf_op jit(solution)/shard_map/ppermute | solution.py:36
  15.5 1.1 %collective-permute-start.7 = (f32[136,128]{1,0:T(8,128)S(1)}, f32[136,128]{1,0:T(8,128)S(1)}, u32[]{:S(2)}, u32[]{:S(2)}) collective-permute-start(f32[136,128]{1,0:T(8,128)S(1)} %slice.6), channel_id=1, source_target_pairs={{0,1},{1,0},{2,3},{3,2},{4,5},{5,4},{6,7},{7,6},{8,9},{9,8},{10,11... | collective-permute-start | bytes 208904 | tf_op jit(solution)/shard_map/ppermute | solution.py:36
  16.7 1.0 %collective-permute-start.12 = (f32[128,128]{1,0:T(8,128)S(1)}, f32[128,128]{1,0:T(8,128)S(1)}, u32[]{:S(2)}, u32[]{:S(2)}) collective-permute-start(f32[128,128]{1,0:T(8,128)S(1)} %slice.7), channel_id=1, source_target_pairs={{0,8},{1,9},{2,10},{3,11},{4,12},{5,13},{6,14},{7,15},{8,0},{9,1},... | collective-permute-start | bytes 196616 | tf_op jit(solution)/shard_map/ppermute | solution.py:36
  17.7 1.1 %collective-permute-done.7 = f32[136,128]{1,0:T(8,128)S(1)} collective-permute-done((f32[136,128]{1,0:T(8,128)S(1)}, f32[136,128]{1,0:T(8,128)S(1)}, u32[]{:S(2)}, u32[]{:S(2)}) %collective-permute-start.7) | collective-permute-done | bytes 69664 | tf_op jit(solution)/shard_map/ppermute | solution.py:36
  18.8 3.8 %collective-permute-start.8 = (f32[136,128]{1,0:T(8,128)S(1)}, f32[136,128]{1,0:T(8,128)S(1)}, u32[]{:S(2)}, u32[]{:S(2)}) collective-permute-start(f32[136,128]{1,0:T(8,128)S(1)} %slice_add_fusion.1), channel_id=1, source_target_pairs={{0,3},{1,2},{2,1},{3,0},{4,7},{5,6},{6,5},{7,4},{8,11},{9,10},{10,... | collective-permute-start | bytes 208904 | tf_op jit(solution)/shard_map/ppermute | solution.py:36
  22.6 2.5 %collective-permute-start.13 = (f32[128,128]{1,0:T(8,128)S(1)}, f32[128,128]{1,0:T(8,128)S(1)}, u32[]{:S(2)}, u32[]{:S(2)}) collective-permute-start(f32[128,128]{1,0:T(8,128)S(1)} %slice_add_fusion), channel_id=1, source_target_pairs={{0,24},{1,25},{2,26},{3,27},{4,28},{5,29},{6,30},{7,31},{8,16},{9,... | collective-permute-start | bytes 196616 | tf_op jit(solution)/shard_map/ppermute | solution.py:36
  25.2 0.0 collective-permute-done.8
  25.2 3.7 %collective-permute-start.9 = (f32[136,128]{1,0:T(8,128)S(1)}, f32[136,128]{1,0:T(8,128)S(1)}, u32[]{:S(2)}, u32[]{:S(2)}) collective-permute-start(f32[136,128]{1,0:T(8,128)S(1)} %add.59), channel_id=1, source_target_pairs={{0,7},{1,6},{2,5},{3,4},{4,3},{5,2},{6,1},{7,0},{8,15},{9,14},{10,... | collective-permute-start | bytes 208904 | tf_op jit(solution)/shard_map/ppermute | solution.py:36
  28.9 0.1 collective-permute-start.14
  29.0 1.9 %collective-permute-done.9 = f32[136,128]{1,0:T(8,128)S(1)} collective-permute-done((f32[136,128]{1,0:T(8,128)S(1)}, f32[136,128]{1,0:T(8,128)S(1)}, u32[]{:S(2)}, u32[]{:S(2)}) %collective-permute-start.9) | collective-permute-done | bytes 69664 | tf_op jit(solution)/shard_map/ppermute | solution.py:36
  30.9 0.8 %collective-permute-start.10 = (f32[136,128]{1,0:T(8,128)S(1)}, f32[136,128]{1,0:T(8,128)S(1)}, u32[]{:S(2)}, u32[]{:S(2)}) collective-permute-start(f32[136,128]{1,0:T(8,128)S(1)} %add.60), channel_id=1, source_target_pairs={{0,8},{1,9},{2,10},{3,11},{4,12},{5,13},{6,14},{7,15},{8,0},{9,1},... | collective-permute-start | bytes 208904 | tf_op jit(solution)/shard_map/ppermute | solution.py:36
  31.7 0.4 collective-permute-done.14
  32.1 1.9 %collective-permute-start.15 = (f32[128,128]{1,0:T(8,128)S(1)}, f32[128,128]{1,0:T(8,128)S(1)}, u32[]{:S(2)}, u32[]{:S(2)}) collective-permute-start(f32[128,128]{1,0:T(8,128)S(1)} %add.65), channel_id=1, source_target_pairs={{0,3},{1,2},{2,1},{3,0},{4,7},{5,6},{6,5},{7,4},{8,11},{9,10},{10,... | collective-permute-start | bytes 196616 | tf_op jit(solution)/shard_map/ppermute | solution.py:36
  34.0 0.4 collective-permute-done.10
  34.5 2.2 %collective-permute-start.11 = (f32[136,128]{1,0:T(8,128)S(1)}, f32[136,128]{1,0:T(8,128)S(1)}, u32[]{:S(2)}, u32[]{:S(2)}) collective-permute-start(f32[136,128]{1,0:T(8,128)S(1)} %add.61), channel_id=1, source_target_pairs={{0,24},{1,25},{2,26},{3,27},{4,28},{5,29},{6,30},{7,31},{8,16},{9,... | collective-permute-start | bytes 208904 | tf_op jit(solution)/shard_map/ppermute | solution.py:36
  36.7 0.9 %collective-permute-done.15 = f32[128,128]{1,0:T(8,128)S(1)} collective-permute-done((f32[128,128]{1,0:T(8,128)S(1)}, f32[128,128]{1,0:T(8,128)S(1)}, u32[]{:S(2)}, u32[]{:S(2)}) %collective-permute-start.15) | collective-permute-done | bytes 65568 | tf_op jit(solution)/shard_map/ppermute | solution.py:36
  37.6 2.5 %collective-permute-start.16 = (f32[128,128]{1,0:T(8,128)S(1)}, f32[128,128]{1,0:T(8,128)S(1)}, u32[]{:S(2)}, u32[]{:S(2)}) collective-permute-start(f32[128,128]{1,0:T(8,128)S(1)} %add.66), channel_id=1, source_target_pairs={{0,7},{1,6},{2,5},{3,4},{4,3},{5,2},{6,1},{7,0},{8,15},{9,14},{10,... | collective-permute-start | bytes 196616 | tf_op jit(solution)/shard_map/ppermute | solution.py:36
  40.1 2.6 %collective-permute-done.16 = f32[128,128]{1,0:T(8,128)S(1)} collective-permute-done((f32[128,128]{1,0:T(8,128)S(1)}, f32[128,128]{1,0:T(8,128)S(1)}, u32[]{:S(2)}, u32[]{:S(2)}) %collective-permute-start.16) | collective-permute-done | bytes 65568 | tf_op jit(solution)/shard_map/ppermute | solution.py:36
  42.7 2.1 %rotation_even.1.turned_even = f32[136,128]{1,0:T(8,128)S(1)} custom-call(f32[136,128]{1,0:T(8,128)S(1)} %add.62.straight), custom_call_target="tpu_custom_call" | custom-call | flops 629145600 | bytes 1048576 | tf_op jit(solution)/shard_map/rotation_even/pallas_call | solution.py:369
  44.8 2.7 %rotation_odd.1.refs_0_ = f32[264,128]{1,0:T(8,128)S(1)} custom-call(f32[136,128]{1,0:T(8,128)S(1)} %add.62.straight, f32[136,128]{1,0:T(8,128)S(1)} %rotation_even.1.turned_even, f32[128,128]{1,0:T(8,128)S(1)} %add.67.crossed), custom_call_target="tpu_custom_call" | custom-call | tf_op jit(solution)/shard_map/rotation_odd/pallas_call | solution.py:378
  47.4 1.6 %collective-permute-start.21 = (f32[264,128]{1,0:T(8,128)S(1)}, f32[264,128]{1,0:T(8,128)S(1)}, u32[]{:S(2)}, u32[]{:S(2)}) collective-permute-start(f32[264,128]{1,0:T(8,128)S(1)} %rotation_odd.1.refs_0_), channel_id=1, source_target_pairs={{0,128},{1,129},{2,130},{3,131},{4,132},{5,133},{6,134},{7,135},{8... | collective-permute-start | bytes 405512 | tf_op jit(solution)/shard_map/ppermute | solution.py:36
  49.1 1.9 %collective-permute-start.19 = (f32[264,128]{1,0:T(8,128)S(1)}, f32[264,128]{1,0:T(8,128)S(1)}, u32[]{:S(2)}, u32[]{:S(2)}) collective-permute-start(f32[264,128]{1,0:T(8,128)S(1)} %rotation_odd.1.refs_0_), channel_id=1, source_target_pairs={{0,64},{1,65},{2,66},{3,67},{4,68},{5,69},{6,70},{7,71},{8,72},{9,... | collective-permute-start | bytes 405512 | tf_op jit(solution)/shard_map/ppermute | solution.py:36
  51.0 0.8 %collective-permute-start.17 = (f32[264,128]{1,0:T(8,128)S(1)}, f32[264,128]{1,0:T(8,128)S(1)}, u32[]{:S(2)}, u32[]{:S(2)}) collective-permute-start(f32[264,128]{1,0:T(8,128)S(1)} %rotation_odd.1.refs_0_), channel_id=1, source_target_pairs={{0,192},{1,193},{2,194},{3,195},{4,196},{5,197},{6,198},{7,199},{8... | collective-permute-start | bytes 405512 | tf_op jit(solution)/shard_map/ppermute | solution.py:36
  51.8 8.8 %collective-permute-start.23 = (f32[264,128]{1,0:T(8,128)S(1)}, f32[264,128]{1,0:T(8,128)S(1)}, u32[]{:S(2)}, u32[]{:S(2)}) collective-permute-start(f32[264,128]{1,0:T(8,128)S(1)} %rotation_odd.1.refs_0_), channel_id=1, source_target_pairs={{0,32},{1,33},{2,34},{3,35},{4,36},{5,37},{6,38},{7,39},{8,40},{9,... | collective-permute-start | bytes 405512 | tf_op jit(solution)/shard_map/ppermute | solution.py:36
  60.6 0.9 %apply_near.4.refs_6_ = f32[256,512]{1,0:T(8,128)S(1)} custom-call(f32[264,128]{1,0:T(8,128)S(1)} %rotation_odd.1.refs_0_, bf16[768,512]{1,0:T(8,128)(2,1)S(1)} %get-tuple-element.58.refs_1_), custom_call_target="tpu_custom_call" | custom-call | flops 402653184 | bytes 1048576 | tf_op jit(solution)/shard_map/apply_near/pallas_call | solution.py:389
  61.5 0.3 collective-permute-start.22
  61.8 1.8 %collective-permute-start.20 = (f32[264,128]{1,0:T(8,128)S(1)}, f32[264,128]{1,0:T(8,128)S(1)}, u32[]{:S(2)}, u32[]{:S(2)}) collective-permute-start(f32[264,128]{1,0:T(8,128)S(1)} %collective-permute-done.19.refs_0_), channel_id=1, source_target_pairs={{0,32},{1,33},{2,34},{3,35},{4,36},{5,37},{6,38},{7,39},{8,40},{9,... | collective-permute-start | bytes 405512 | tf_op jit(solution)/shard_map/ppermute | solution.py:36
  63.6 0.0 collective-permute-done.17.refs_0_
  63.6 0.6 collective-permute-start.18
  64.2 0.9 %apply_near.6.refs_8_ = f32[256,512]{1,0:T(8,128)S(1)} custom-call(f32[264,128]{1,0:T(8,128)S(1)} %collective-permute-done.17.refs_0_, bf16[768,512]{1,0:T(8,128)(2,1)S(1)} %get-tuple-element.60.refs_1_), custom_call_target="tpu_custom_call" | custom-call | flops 402653184 | bytes 1048576 | tf_op jit(solution)/shard_map/apply_near/pallas_call | solution.py:389
  65.0 0.0 collective-permute-done.23.refs_0_
  65.1 0.9 %apply_near.5.refs_7_ = f32[256,512]{1,0:T(8,128)S(1)} custom-call(f32[264,128]{1,0:T(8,128)S(1)} %collective-permute-done.23.refs_0_, bf16[768,512]{1,0:T(8,128)(2,1)S(1)} %get-tuple-element.59.refs_1_), custom_call_target="tpu_custom_call" | custom-call | flops 402653184 | bytes 1048576 | tf_op jit(solution)/shard_map/apply_near/pallas_call | solution.py:389
  65.9 1.5 %apply_near.7 = (f32[256,512]{1,0:T(8,128)S(1)}, f32[256,512]{1,0:T(8,128)S(1)}) custom-call(f32[264,128]{1,0:T(8,128)S(1)} %collective-permute-done.19.refs_0_, f32[264,128]{1,0:T(8,128)S(1)} %collective-permute-done.21.refs_1_, bf16[768,512]{1,0:T(8,128)(2,1)S(1)} %get-tuple-element.61.refs_2_, bf16[768,512]{1,0:T(8,128)(2,1)S(1)} %get-tuple-element.62.refs_3_), custom_call_target="tpu_custom_call" | custom-call | flops 805306368 | bytes 2097152 | tf_op jit(solution)/shard_map/apply_near/pallas_call | solution.py:389
  67.4 4.2 %apply_far.1 = f32[2048,512]{1,0:T(8,128)} custom-call(s32[32]{0:T(128)} %seating.3, f32[264,128]{1,0:T(8,128)S(1)} %collective-permute-done.18.refs_0_, f32[264,128]{1,0:T(8,128)S(1)} %collective-permute-done.20.refs_1_, f32[264,128]{1,0:T(8,128)S(1)} %collective-permute-done.22.refs_2_, bf16[768,512]{1,0:T(8,128)(2,1)S(1)} %get-tuple-element.55.refs_3_, ...), custom_call_target="tpu_custom_call" | custom-call | tf_op jit(solution)/shard_map/apply_far/pallas_call | solution.py:411
  (26 shorter events, 0.2 us)
Async XLA Ops:
  3.5 4.8 %collective-permute-start.3 = (f32[264,128]{1,0:T(8,128)S(1)}, f32[264,128]{1,0:T(8,128)S(1)}, u32[]{:S(2)}, u32[]{:S(2)}) collective-permute-start(f32[264,128]{1,0:T(8,128)S(1)} %get-tuple-element.41), channel_id=1, source_target_pairs={{0,32},{1,33},{2,34},{3,35},{4,36},{5,37},{6,38},{7,39},{8,40},{9,... | collective-permute-start | bytes 405512 | tf_op jit(solution)/shard_map/ppermute | solution.py:36
  6.8 2.6 %collective-permute-start.1 = (f32[264,128]{1,0:T(8,128)S(1)}, f32[264,128]{1,0:T(8,128)S(1)}, u32[]{:S(2)}, u32[]{:S(2)}) collective-permute-start(f32[264,128]{1,0:T(8,128)S(1)} %get-tuple-element.39), channel_id=1, source_target_pairs={{0,32},{1,33},{2,34},{3,35},{4,36},{5,37},{6,38},{7,39},{8,40},{9,... | collective-permute-start | bytes 405512 | tf_op jit(solution)/shard_map/ppermute | solution.py:36
  6.9 3.0 %collective-permute-start.5 = (f32[264,128]{1,0:T(8,128)S(1)}, f32[264,128]{1,0:T(8,128)S(1)}, u32[]{:S(2)}, u32[]{:S(2)}) collective-permute-start(f32[264,128]{1,0:T(8,128)S(1)} %get-tuple-element.44), channel_id=1, source_target_pairs={{0,32},{1,33},{2,34},{3,35},{4,36},{5,37},{6,38},{7,39},{8,40},{9,... | collective-permute-start | bytes 405512 | tf_op jit(solution)/shard_map/ppermute | solution.py:36
  7.3 6.2 %collective-permute-start = (f32[264,128]{1,0:T(8,128)S(1)}, f32[264,128]{1,0:T(8,128)S(1)}, u32[]{:S(2)}, u32[]{:S(2)}) collective-permute-start(f32[264,128]{1,0:T(8,128)S(1)} %get-tuple-element.37), channel_id=1, source_target_pairs={{0,32},{1,33},{2,34},{3,35},{4,36},{5,37},{6,38},{7,39},{8,40},{9,... | collective-permute-start | bytes 405512 | tf_op jit(solution)/shard_map/ppermute | solution.py:36
  8.3 5.7 %collective-permute-start.4 = (f32[264,128]{1,0:T(8,128)S(1)}, f32[264,128]{1,0:T(8,128)S(1)}, u32[]{:S(2)}, u32[]{:S(2)}) collective-permute-start(f32[264,128]{1,0:T(8,128)S(1)} %add.54), channel_id=1, source_target_pairs={{0,128},{1,129},{2,130},{3,131},{4,132},{5,133},{6,134},{7,135},{8... | collective-permute-start | bytes 405512 | tf_op jit(solution)/shard_map/ppermute | solution.py:36
  9.4 6.0 %collective-permute-start.2 = (f32[264,128]{1,0:T(8,128)S(1)}, f32[264,128]{1,0:T(8,128)S(1)}, u32[]{:S(2)}, u32[]{:S(2)}) collective-permute-start(f32[264,128]{1,0:T(8,128)S(1)} %add.52), channel_id=1, source_target_pairs={{0,64},{1,65},{2,66},{3,67},{4,68},{5,69},{6,70},{7,71},{8,72},{9,... | collective-permute-start | bytes 405512 | tf_op jit(solution)/shard_map/ppermute | solution.py:36
  9.8 5.6 %collective-permute-start.6 = (f32[264,128]{1,0:T(8,128)S(1)}, f32[264,128]{1,0:T(8,128)S(1)}, u32[]{:S(2)}, u32[]{:S(2)}) collective-permute-start(f32[264,128]{1,0:T(8,128)S(1)} %add.56), channel_id=1, source_target_pairs={{0,192},{1,193},{2,194},{3,195},{4,196},{5,197},{6,198},{7,199},{8... | collective-permute-start | bytes 405512 | tf_op jit(solution)/shard_map/ppermute | solution.py:36
  15.5 3.2 %collective-permute-start.7 = (f32[136,128]{1,0:T(8,128)S(1)}, f32[136,128]{1,0:T(8,128)S(1)}, u32[]{:S(2)}, u32[]{:S(2)}) collective-permute-start(f32[136,128]{1,0:T(8,128)S(1)} %slice.6), channel_id=1, source_target_pairs={{0,1},{1,0},{2,3},{3,2},{4,5},{5,4},{6,7},{7,6},{8,9},{9,8},{10,11... | collective-permute-start | bytes 208904 | tf_op jit(solution)/shard_map/ppermute | solution.py:36
  16.7 6.0 %collective-permute-start.12 = (f32[128,128]{1,0:T(8,128)S(1)}, f32[128,128]{1,0:T(8,128)S(1)}, u32[]{:S(2)}, u32[]{:S(2)}) collective-permute-start(f32[128,128]{1,0:T(8,128)S(1)} %slice.7), channel_id=1, source_target_pairs={{0,8},{1,9},{2,10},{3,11},{4,12},{5,13},{6,14},{7,15},{8,0},{9,1},... | collective-permute-start | bytes 196616 | tf_op jit(solution)/shard_map/ppermute | solution.py:36
  18.8 6.4 %collective-permute-start.8 = (f32[136,128]{1,0:T(8,128)S(1)}, f32[136,128]{1,0:T(8,128)S(1)}, u32[]{:S(2)}, u32[]{:S(2)}) collective-permute-start(f32[136,128]{1,0:T(8,128)S(1)} %slice_add_fusion.1), channel_id=1, source_target_pairs={{0,3},{1,2},{2,1},{3,0},{4,7},{5,6},{6,5},{7,4},{8,11},{9,10},{10,... | collective-permute-start | bytes 208904 | tf_op jit(solution)/shard_map/ppermute | solution.py:36
  22.6 6.3 %collective-permute-start.13 = (f32[128,128]{1,0:T(8,128)S(1)}, f32[128,128]{1,0:T(8,128)S(1)}, u32[]{:S(2)}, u32[]{:S(2)}) collective-permute-start(f32[128,128]{1,0:T(8,128)S(1)} %slice_add_fusion), channel_id=1, source_target_pairs={{0,24},{1,25},{2,26},{3,27},{4,28},{5,29},{6,30},{7,31},{8,16},{9,... | collective-permute-start | bytes 196616 | tf_op jit(solution)/shard_map/ppermute | solution.py:36
  25.2 5.7 %collective-permute-start.9 = (f32[136,128]{1,0:T(8,128)S(1)}, f32[136,128]{1,0:T(8,128)S(1)}, u32[]{:S(2)}, u32[]{:S(2)}) collective-permute-start(f32[136,128]{1,0:T(8,128)S(1)} %add.59), channel_id=1, source_target_pairs={{0,7},{1,6},{2,5},{3,4},{4,3},{5,2},{6,1},{7,0},{8,15},{9,14},{10,... | collective-permute-start | bytes 208904 | tf_op jit(solution)/shard_map/ppermute | solution.py:36
  28.9 3.2 %collective-permute-start.14 = (f32[128,128]{1,0:T(8,128)S(1)}, f32[128,128]{1,0:T(8,128)S(1)}, u32[]{:S(2)}, u32[]{:S(2)}) collective-permute-start(f32[128,128]{1,0:T(8,128)S(1)} %add.64), channel_id=1, source_target_pairs={{0,1},{1,0},{2,3},{3,2},{4,5},{5,4},{6,7},{7,6},{8,9},{9,8},{10,11... | collective-permute-start | bytes 196616 | tf_op jit(solution)/shard_map/ppermute | solution.py:36
  30.9 3.5 %collective-permute-start.10 = (f32[136,128]{1,0:T(8,128)S(1)}, f32[136,128]{1,0:T(8,128)S(1)}, u32[]{:S(2)}, u32[]{:S(2)}) collective-permute-start(f32[136,128]{1,0:T(8,128)S(1)} %add.60), channel_id=1, source_target_pairs={{0,8},{1,9},{2,10},{3,11},{4,12},{5,13},{6,14},{7,15},{8,0},{9,1},... | collective-permute-start | bytes 208904 | tf_op jit(solution)/shard_map/ppermute | solution.py:36
  32.1 5.4 %collective-permute-start.15 = (f32[128,128]{1,0:T(8,128)S(1)}, f32[128,128]{1,0:T(8,128)S(1)}, u32[]{:S(2)}, u32[]{:S(2)}) collective-permute-start(f32[128,128]{1,0:T(8,128)S(1)} %add.65), channel_id=1, source_target_pairs={{0,3},{1,2},{2,1},{3,0},{4,7},{5,6},{6,5},{7,4},{8,11},{9,10},{10,... | collective-permute-start | bytes 196616 | tf_op jit(solution)/shard_map/ppermute | solution.py:36
  34.5 8.2 %collective-permute-start.11 = (f32[136,128]{1,0:T(8,128)S(1)}, f32[136,128]{1,0:T(8,128)S(1)}, u32[]{:S(2)}, u32[]{:S(2)}) collective-permute-start(f32[136,128]{1,0:T(8,128)S(1)} %add.61), channel_id=1, source_target_pairs={{0,24},{1,25},{2,26},{3,27},{4,28},{5,29},{6,30},{7,31},{8,16},{9,... | collective-permute-start | bytes 208904 | tf_op jit(solution)/shard_map/ppermute | solution.py:36
  37.6 5.0 %collective-permute-start.16 = (f32[128,128]{1,0:T(8,128)S(1)}, f32[128,128]{1,0:T(8,128)S(1)}, u32[]{:S(2)}, u32[]{:S(2)}) collective-permute-start(f32[128,128]{1,0:T(8,128)S(1)} %add.66), channel_id=1, source_target_pairs={{0,7},{1,6},{2,5},{3,4},{4,3},{5,2},{6,1},{7,0},{8,15},{9,14},{10,... | collective-permute-start | bytes 196616 | tf_op jit(solution)/shard_map/ppermute | solution.py:36
  47.4 14.0 %collective-permute-start.21 = (f32[264,128]{1,0:T(8,128)S(1)}, f32[264,128]{1,0:T(8,128)S(1)}, u32[]{:S(2)}, u32[]{:S(2)}) collective-permute-start(f32[264,128]{1,0:T(8,128)S(1)} %rotation_odd.1.refs_0_), channel_id=1, source_target_pairs={{0,128},{1,129},{2,130},{3,131},{4,132},{5,133},{6,134},{7,135},{8... | collective-permute-start | bytes 405512 | tf_op jit(solution)/shard_map/ppermute | solution.py:36
  49.1 12.7 %collective-permute-start.19 = (f32[264,128]{1,0:T(8,128)S(1)}, f32[264,128]{1,0:T(8,128)S(1)}, u32[]{:S(2)}, u32[]{:S(2)}) collective-permute-start(f32[264,128]{1,0:T(8,128)S(1)} %rotation_odd.1.refs_0_), channel_id=1, source_target_pairs={{0,64},{1,65},{2,66},{3,67},{4,68},{5,69},{6,70},{7,71},{8,72},{9,... | collective-permute-start | bytes 405512 | tf_op jit(solution)/shard_map/ppermute | solution.py:36
  51.0 12.6 %collective-permute-start.17 = (f32[264,128]{1,0:T(8,128)S(1)}, f32[264,128]{1,0:T(8,128)S(1)}, u32[]{:S(2)}, u32[]{:S(2)}) collective-permute-start(f32[264,128]{1,0:T(8,128)S(1)} %rotation_odd.1.refs_0_), channel_id=1, source_target_pairs={{0,192},{1,193},{2,194},{3,195},{4,196},{5,197},{6,198},{7,199},{8... | collective-permute-start | bytes 405512 | tf_op jit(solution)/shard_map/ppermute | solution.py:36
  51.8 13.3 %collective-permute-start.23 = (f32[264,128]{1,0:T(8,128)S(1)}, f32[264,128]{1,0:T(8,128)S(1)}, u32[]{:S(2)}, u32[]{:S(2)}) collective-permute-start(f32[264,128]{1,0:T(8,128)S(1)} %rotation_odd.1.refs_0_), channel_id=1, source_target_pairs={{0,32},{1,33},{2,34},{3,35},{4,36},{5,37},{6,38},{7,39},{8,40},{9,... | collective-permute-start | bytes 405512 | tf_op jit(solution)/shard_map/ppermute | solution.py:36
  61.5 5.9 %collective-permute-start.22 = (f32[264,128]{1,0:T(8,128)S(1)}, f32[264,128]{1,0:T(8,128)S(1)}, u32[]{:S(2)}, u32[]{:S(2)}) collective-permute-start(f32[264,128]{1,0:T(8,128)S(1)} %collective-permute-done.21.refs_1_), channel_id=1, source_target_pairs={{0,32},{1,33},{2,34},{3,35},{4,36},{5,37},{6,38},{7,39},{8,40},{9,... | collective-permute-start | bytes 405512 | tf_op jit(solution)/shard_map/ppermute | solution.py:36
  61.8 5.6 %collective-permute-start.20 = (f32[264,128]{1,0:T(8,128)S(1)}, f32[264,128]{1,0:T(8,128)S(1)}, u32[]{:S(2)}, u32[]{:S(2)}) collective-permute-start(f32[264,128]{1,0:T(8,128)S(1)} %collective-permute-done.19.refs_0_), channel_id=1, source_target_pairs={{0,32},{1,33},{2,34},{3,35},{4,36},{5,37},{6,38},{7,39},{8,40},{9,... | collective-permute-start | bytes 405512 | tf_op jit(solution)/shard_map/ppermute | solution.py:36
  63.6 3.8 %collective-permute-start.18 = (f32[264,128]{1,0:T(8,128)S(1)}, f32[264,128]{1,0:T(8,128)S(1)}, u32[]{:S(2)}, u32[]{:S(2)}) collective-permute-start(f32[264,128]{1,0:T(8,128)S(1)} %collective-permute-done.17.refs_0_), channel_id=1, source_target_pairs={{0,32},{1,33},{2,34},{3,35},{4,36},{5,37},{6,38},{7,39},{8,40},{9,... | collective-permute-start | bytes 405512 | tf_op jit(solution)/shard_map/ppermute | solution.py:36
